TPU v7x, 32 devices: a whole 2x2x4 slice. The times are simulated.
32 devices in a mesh: seq: 16 (over z, x, core), chan: 2 (over y).
Axes of the slice: x: 2, y: 2, z: 4, core: 2. Of those that a mesh axis runs over, the one named last changes fastest.
Arguments:
- inputs: bfloat16 [4096, 2048], P('chan', 'seq'), may hold values from -6 to 6
- gating: bfloat16 [4096, 2048], P('chan', 'seq'), may hold values from -6 to 6
- grad_out: bfloat16 [4096, 2048], P('chan', 'seq'), may hold values from -6 to 6
- filters: float32 [64, 2048], P(None, ('seq', 'chan')), as said below
Outputs:
- grad_inputs: bfloat16 [4096, 2048], P('chan', 'seq')
- grad_gating: bfloat16 [4096, 2048], P('chan', 'seq')
- grad_filters: float32 [64, 2048], P(None, ('seq', 'chan'))
Inputs may be any that keep to these rules, and one draw needn't show every extreme that they name: `filters`: every entry's magnitude is at most 0.77 times the square root of 131072.
All inputs are finite; a program needn't handle non-finite values.
Results may differ from a plain program's by a relative error of at most 0.0049.
Values may be sent and summed in bfloat16 or wider, within the bound.
A program may use at most 64 MiB of HBM per device.

v0:
```python
import math

import jax
import jax.numpy as jnp
from jax import lax
from jax.sharding import PartitionSpec as P

D = 4096
G = 64


HIGHEST = lax.Precision.HIGHEST


def make_tables(seq_count, block_len):
    outer = 2 * seq_count
    total = outer * block_len
    outer_index = jnp.arange(outer, dtype=jnp.int32)
    block_index = jnp.arange(seq_count, dtype=jnp.int32)
    inner_index = jnp.arange(block_len, dtype=jnp.int32)
    block_angle = (outer_index[:, None] * block_index[None, :] % outer).astype(jnp.float32) * (
        2.0 * math.pi / outer
    )
    twist_angle = (outer_index[:, None] * inner_index[None, :] % total).astype(jnp.float32) * (
        2.0 * math.pi / total
    )
    inner_angle = (inner_index[:, None] * inner_index[None, :] % block_len).astype(jnp.float32) * (
        2.0 * math.pi / block_len
    )
    return (
        jnp.cos(block_angle),
        jnp.sin(block_angle),
        jnp.cos(twist_angle),
        jnp.sin(twist_angle),
        jnp.cos(inner_angle),
        jnp.sin(inner_angle),
    )


def right_product(values, table):
    return jnp.einsum("ckm,mj->ckj", values, table, precision=HIGHEST)


def forward_dft(signal, tables):
    block_cos, block_sin, twist_cos, twist_sin, inner_cos, inner_sin = tables
    real_first = jnp.einsum("kn,cnm->ckm", block_cos, signal, precision=HIGHEST)
    imag_first = -jnp.einsum("kn,cnm->ckm", block_sin, signal, precision=HIGHEST)
    real_twist = real_first * twist_cos + imag_first * twist_sin
    imag_twist = imag_first * twist_cos - real_first * twist_sin
    real_spec = right_product(real_twist, inner_cos) + right_product(imag_twist, inner_sin)
    imag_spec = right_product(imag_twist, inner_cos) - right_product(real_twist, inner_sin)
    return (real_spec, imag_spec)


def inverse_dft(real_spec, imag_spec, tables):
    block_cos, block_sin, twist_cos, twist_sin, inner_cos, inner_sin = tables
    real_first = right_product(real_spec, inner_cos) - right_product(imag_spec, inner_sin)
    imag_first = right_product(real_spec, inner_sin) + right_product(imag_spec, inner_cos)
    real_twist = real_first * twist_cos - imag_first * twist_sin
    imag_twist = real_first * twist_sin + imag_first * twist_cos
    total = real_spec.shape[1] * real_spec.shape[2]
    result = jnp.einsum("kn,ckm->cnm", block_cos, real_twist, precision=HIGHEST)
    result = result - jnp.einsum("kn,ckm->cnm", block_sin, imag_twist, precision=HIGHEST)
    return result / total


def shards(inputs, gating, grad_out, filters):
    seq_count = lax.axis_size("seq")
    chan_count = lax.axis_size("chan")
    chan_rows, block_len = inputs.shape
    local_chan = chan_rows // seq_count
    group_width = D // G
    groups_here = G // chan_count
    local_groups = max(1, local_chan // group_width)
    group_share = local_chan // local_groups
    copies = max(1, seq_count // groups_here)
    length = block_len * seq_count
    outer = 2 * seq_count
    factor = 1.0 / math.sqrt(group_width * length)
    tables = make_tables(seq_count, block_len)
    whole = lax.all_gather(filters, ("seq", "chan"), axis=1, tiled=True)
    first_group = (
        lax.axis_index("chan") * chan_rows + lax.axis_index("seq") * local_chan
    ) // group_width
    kernel_rows = lax.dynamic_slice_in_dim(whole, first_group, local_groups, 0)
    kernel_blocks = kernel_rows.reshape(local_groups, seq_count, block_len)
    kernel_real, kernel_imag = forward_dft(kernel_blocks * factor, tables)
    kernel_real = kernel_real[:, None]
    kernel_imag = kernel_imag[:, None]
    shaped_inputs = inputs.reshape(chan_rows, 1, block_len)
    values, gate_part, upstream = (
        lax.all_to_all(shaped_inputs, "seq", split_axis=0, concat_axis=1, tiled=True),
        lax.all_to_all(
            gating.reshape(chan_rows, 1, block_len), "seq", split_axis=0, concat_axis=1, tiled=True
        ),
        lax.all_to_all(
            grad_out.reshape(chan_rows, 1, block_len),
            "seq",
            split_axis=0,
            concat_axis=1,
            tiled=True,
        ),
    )
    input_real, input_imag = forward_dft(values.astype(jnp.float32), tables)
    upstream_f = upstream.astype(jnp.float32)
    product_b = lax.optimization_barrier(
        (gate_part.astype(jnp.float32) * upstream_f).astype(jnp.bfloat16)
    )
    up_real, up_imag = forward_dft(product_b.astype(jnp.float32), tables)
    grouped_shape = (local_groups, group_share, outer, block_len)
    input_real = input_real.reshape(grouped_shape)
    input_imag = input_imag.reshape(grouped_shape)
    up_real = up_real.reshape(grouped_shape)
    up_imag = up_imag.reshape(grouped_shape)
    flat_shape = (local_chan, outer, block_len)
    conv_real = input_real * kernel_real - input_imag * kernel_imag
    conv_imag = input_real * kernel_imag + input_imag * kernel_real
    convolved = inverse_dft(conv_real.reshape(flat_shape), conv_imag.reshape(flat_shape), tables)
    conv_b = convolved.astype(jnp.bfloat16)
    second = (upstream_f * lax.optimization_barrier(conv_b).astype(jnp.float32)).astype(
        jnp.bfloat16
    )
    back_real = up_real * kernel_real + up_imag * kernel_imag
    back_imag = up_imag * kernel_real - up_real * kernel_imag
    grad_input = inverse_dft(
        back_real.reshape(flat_shape), back_imag.reshape(flat_shape), tables
    ).astype(jnp.bfloat16)
    returned_input, returned_second = (
        lax.all_to_all(grad_input, "seq", split_axis=1, concat_axis=0, tiled=True),
        lax.all_to_all(second, "seq", split_axis=1, concat_axis=0, tiled=True),
    )
    returned_second = returned_second.reshape(chan_rows, block_len)
    cross_real = jnp.sum(input_real * up_real + input_imag * up_imag, axis=1)
    cross_imag = jnp.sum(input_real * up_imag - input_imag * up_real, axis=1)
    partial_grad = inverse_dft(cross_real, cross_imag, tables) * factor
    received = lax.all_to_all(partial_grad, "seq", split_axis=1, concat_axis=0, tiled=True)
    summed = received.reshape(groups_here, copies, block_len).sum(axis=1)
    grad_filters = lax.all_to_all(summed, "chan", split_axis=1, concat_axis=0, tiled=True)
    return (returned_input.reshape(chan_rows, block_len), returned_second, grad_filters)


def solution(mesh):
    placed = (P("chan", "seq"), P("chan", "seq"), P("chan", "seq"), P(None, ("seq", "chan")))
    return jax.shard_map(
        shards,
        mesh=mesh,
        in_specs=placed,
        out_specs=(P("chan", "seq"), P("chan", "seq"), P(None, ("seq", "chan"))),
        check_vma=False,
    )
```

profile of v0, /device:TPU:0, one launch (start us, length us, event | category | flops | bytes accessed | tf_op | source)
XLA Modules:
  0.0 250.7 jit_solution(15705486091297072414)
XLA Ops:
  0.6 0.5 broadcast.240
  1.2 2.1 reduce
  3.2 0.9 reshape.117
  4.1 7.4 %all-to-all-start.3 = ((bf16[16,2,8192]{2,1,0:T(2,128)(2,1)}), bf16[16,2,8192]{2,1,0:T(2,128)(2,1)S(1)}, u32[]{:S(2)}, u32[]{:S(2)}) async-start(bf16[16,2,8192]{2,1,0:T(2,128)(2,1)} %reshape.117), calls=%async_computation.3 | async-start | bytes 1048576 | tf_op jit(solution)/shard_map/all_to_all | solution.py:92
  11.6 76.8 %all_gather.3 = f32[64,2048]{0,1:T(8,128)S(1)} all-gather(f32[64,64]{0,1:T(8,128)S(1)} %copy.151), channel_id=1, replica_groups=mesh['seq'=16,'chan'=2] {'seq','chan'}, dimensions={1}, use_global_device_ids=true | all-gather | bytes 540672 | tf_op jit(solution)/shard_map/all_gather | solution.py:81
  89.8 0.4 fusion.149
  90.3 0.4 convolution_add_fusion.1
  90.8 0.4 fusion.146
  91.2 0.4 convolution_subtract_fusion.1
  91.7 1.0 reduce.2
  92.7 0.9 reshape.113
  93.7 1.0 reduce.1
  94.7 0.9 reshape.115
  95.6 3.6 %all-to-all-start = ((bf16[16,2,8192]{2,1,0:T(2,128)(2,1)}), bf16[16,2,8192]{2,1,0:T(2,128)(2,1)S(1)}, u32[]{:S(2)}, u32[]{:S(2)}) async-start(bf16[16,2,8192]{2,1,0:T(2,128)(2,1)} %reshape.113), calls=%async_computation | async-start | bytes 1048576 | tf_op jit(solution)/shard_map/all_to_all | solution.py:93
  99.2 0.7 reshape.118
  100.0 1.1 fusion.115
  101.1 1.5 add_bitcast_fusion
  102.6 3.6 %fusion.38 = f32[128,32,128]{2,0,1:T(8,128)S(1)} fusion(f32[128,32,128]{2,1,0:T(8,128)S(1)} %get-tuple-element.10), kind=kOutput, calls=%fused_computation.56 | convolution fusion | flops 805535744 | bytes 4194304 | tf_op jit(solution)/shard_map/ckm,mj->ckj/dot_general | solution.py:41
  106.2 3.6 %fusion.40 = f32[128,32,128]{2,0,1:T(8,128)S(1)} fusion(f32[128,32,128]{2,1,0:T(8,128)S(1)} %get-tuple-element.10), kind=kOutput, calls=%fused_computation.58 | convolution fusion | flops 805535744 | bytes 4194304 | tf_op jit(solution)/shard_map/ckm,mj->ckj/dot_general | solution.py:41
  109.8 3.8 %fusion.63 = f32[128,32,128]{2,0,1:T(8,128)S(1)} fusion(f32[128,32,128]{2,0,1:T(8,128)S(1)} %fusion.38, f32[128,32,128]{2,1,0:T(8,128)S(1)} %get-tuple-element.9), kind=kOutput, calls=%fused_computation.75 | convolution fusion | flops 806060032 | bytes 6291456 | tf_op jit(solution)/shard_map/ckm,mj->ckj/dot_general | solution.py:41
  113.6 5.3 %fusion.2 = (f32[128,32,128]{2,0,1:T(8,128)S(1)}, f32[128,32,128]{2,0,1:T(8,128)S(1)}, f32[128,32,128]{2,0,1:T(8,128)}) fusion(f32[128,32,128]{2,0,1:T(8,128)S(1)} %fusion.63, f32[2,32,128]{2,0,1:T(2,128)S(1)} %copy.156, f32[2,32,128]{2,0,1:T(2,128)S(1)} %copy.153, f32[128,32,128]{2,0,1:T(8,128)S(1)} %fusion.40, f32[128,32,128]{2,1,0:T(8,128)S(1)} %get-tuple-element.9), kind=kOutput, calls=%fused_computation.10 | convolution fusion | flops 809205760 | bytes 12648448 | tf_op jit(solution)/shard_map/ckm,mj->ckj/dot_general | solution.py:41
  119.0 3.3 %fusion.24 = f32[128,32,128]{2,1,0:T(8,128)S(1)} fusion(f32[128,32,128]{2,0,1:T(8,128)S(1)} %get-tuple-element.6), kind=kOutput, calls=%fused_computation.42 | convolution fusion | flops 805535744 | bytes 4194304 | tf_op jit(solution)/shard_map/ckm,mj->ckj/dot_general | solution.py:41
  122.3 5.0 %fusion.22 = f32[128,32,128]{2,1,0:T(8,128)} fusion(f32[128,32,128]{2,0,1:T(8,128)S(1)} %get-tuple-element.6), kind=kOutput, calls=%fused_computation.40 | convolution fusion | flops 805535744 | bytes 4194304 | tf_op jit(solution)/shard_map/ckm,mj->ckj/dot_general | solution.py:41
  127.3 4.7 %fusion.72 = f32[128,32,128]{2,1,0:T(8,128)} fusion(f32[128,32,128]{2,1,0:T(8,128)S(1)} %fusion.24, f32[128,32,128]{2,0,1:T(8,128)S(1)} %get-tuple-element.5), kind=kOutput, calls=%fused_computation.78 | convolution fusion | flops 806060032 | bytes 6291456 | tf_op jit(solution)/shard_map/ckm,mj->ckj/dot_general | solution.py:41
  132.0 6.0 %all-to-all-start.1 = ((bf16[16,2,8192]{2,1,0:T(2,128)(2,1)}), bf16[16,2,8192]{2,1,0:T(2,128)(2,1)S(1)}, u32[]{:S(2)}, u32[]{:S(2)}) async-start(bf16[16,2,8192]{2,1,0:T(2,128)(2,1)} %reshape.115), calls=%async_computation.1 | async-start | bytes 1048576 | tf_op jit(solution)/shard_map/all_to_all | solution.py:96
  138.0 5.1 %fusion.75 = f32[128,32,128]{2,1,0:T(8,128)S(1)} fusion(f32[128,32,128]{2,1,0:T(8,128)} %fusion.22, f32[128,32,128]{2,0,1:T(8,128)S(1)} %get-tuple-element.5), kind=kOutput, calls=%fused_computation.79 | convolution fusion | flops 806060032 | bytes 6291456 | tf_op jit(solution)/shard_map/ckm,mj->ckj/dot_general | solution.py:41
  143.2 1.5 fusion.6
  144.6 2.3 fusion.96
  147.0 0.5 reshape.114
  147.7 4.6 %all-to-all-done.1 = bf16[16,2,8192]{2,1,0:T(2,128)(2,1)S(1)} async-done(((bf16[16,2,8192]{2,1,0:T(2,128)(2,1)}), bf16[16,2,8192]{2,1,0:T(2,128)(2,1)S(1)}, u32[]{:S(2)}, u32[]{:S(2)}) %all-to-all-start.1) | async-done | bytes 524320 | tf_op jit(solution)/shard_map/all_to_all | solution.py:96
  152.3 0.7 reshape.116
  153.2 1.3 fusion.106
  154.4 1.1 fusion.214
  155.5 1.5 fusion.4
  157.0 3.6 %fusion.46 = f32[128,32,128]{2,0,1:T(8,128)S(1)} fusion(f32[128,32,128]{2,1,0:T(8,128)S(1)} %get-tuple-element.12), kind=kOutput, calls=%fused_computation.64 | convolution fusion | flops 805535744 | bytes 4194304 | tf_op jit(solution)/shard_map/ckm,mj->ckj/dot_general | solution.py:41
  160.6 3.6 %fusion.48 = f32[128,32,128]{2,0,1:T(8,128)S(1)} fusion(f32[128,32,128]{2,1,0:T(8,128)S(1)} %get-tuple-element.12), kind=kOutput, calls=%fused_computation.66 | convolution fusion | flops 805535744 | bytes 4194304 | tf_op jit(solution)/shard_map/ckm,mj->ckj/dot_general | solution.py:41
  164.2 4.0 %fusion.57 = f32[128,32,128]{2,0,1:T(8,128)S(1)} fusion(f32[128,32,128]{2,0,1:T(8,128)S(1)} %fusion.46, f32[128,32,128]{2,1,0:T(8,128)S(1)} %get-tuple-element.11), kind=kOutput, calls=%fused_computation.73 | convolution fusion | flops 806060032 | bytes 6291456 | tf_op jit(solution)/shard_map/ckm,mj->ckj/dot_general | solution.py:41
  168.3 4.0 %fusion = (f32[128,32,128]{2,0,1:T(8,128)S(1)}, f32[128,32,128]{2,0,1:T(8,128)S(1)}, f32[128,32,128]{2,0,1:T(8,128)S(1)}) fusion(f32[128,32,128]{2,0,1:T(8,128)S(1)} %fusion.57, f32[2,32,128]{2,0,1:T(2,128)S(1)} %copy.156, f32[2,32,128]{2,0,1:T(2,128)S(1)} %copy.153, f32[128,32,128]{2,0,1:T(8,128)S(1)} %fusion.48, f32[128,32,128]{2,1,0:T(8,128)S(1)} %get-tuple-element.11), kind=kOutput, calls=%fused_computation.8 | convolution fusion | flops 809205760 | bytes 12648448 | tf_op jit(solution)/shard_map/ckm,mj->ckj/dot_general | solution.py:41
  172.3 1.4 bitcast_reduce_fusion
  174.1 0.4 fusion.124
  174.6 4.8 %fusion.32 = f32[128,32,128]{2,1,0:T(8,128)} fusion(f32[128,32,128]{2,0,1:T(8,128)S(1)} %get-tuple-element.8), kind=kOutput, calls=%fused_computation.50 | convolution fusion | flops 805535744 | bytes 4194304 | tf_op jit(solution)/shard_map/ckm,mj->ckj/dot_general | solution.py:41
  179.3 4.6 %fusion.30 = f32[128,32,128]{2,1,0:T(8,128)} fusion(f32[128,32,128]{2,0,1:T(8,128)S(1)} %get-tuple-element.8), kind=kOutput, calls=%fused_computation.48 | convolution fusion | flops 805535744 | bytes 4194304 | tf_op jit(solution)/shard_map/ckm,mj->ckj/dot_general | solution.py:41
  183.9 0.4 convolution_subtract_fusion
  184.4 0.4 convolution_add_fusion
  185.2 0.6 copy.177
  185.9 4.2 %all-to-all-start.5 = ((f32[2,16,128]{2,0,1:T(2,128)}), f32[2,16,128]{2,0,1:T(2,128)S(1)}, u32[]{:S(2)}, u32[]{:S(2)}) async-start(f32[2,16,128]{2,0,1:T(2,128)} %copy.177), calls=%async_computation.5 | async-start | bytes 32768 | tf_op jit(solution)/shard_map/all_to_all | solution.py:136
  190.0 5.1 %fusion.66 = f32[128,32,128]{2,1,0:T(8,128)S(1)} fusion(f32[128,32,128]{2,1,0:T(8,128)} %fusion.32, f32[128,32,128]{2,0,1:T(8,128)S(1)} %get-tuple-element.7), kind=kOutput, calls=%fused_computation.76 | convolution fusion | flops 806060032 | bytes 6291456 | tf_op jit(solution)/shard_map/ckm,mj->ckj/dot_general | solution.py:41
  195.2 3.4 %fusion.69 = f32[128,32,128]{2,1,0:T(8,128)S(1)} fusion(f32[128,32,128]{2,1,0:T(8,128)S(1)} %copy-done.5, f32[128,32,128]{2,0,1:T(8,128)S(1)} %get-tuple-element.7), kind=kOutput, calls=%fused_computation.77 | convolution fusion | flops 806060032 | bytes 6291456 | tf_op jit(solution)/shard_map/ckm,mj->ckj/dot_general | solution.py:41
  198.6 1.3 copy-done.1
  199.9 1.5 fusion.14
  201.5 0.7 reshape.119
  202.2 3.3 %all-to-all-start.6 = ((f32[2,1,2048]{2,1,0:T(1,128)}), f32[2,1,2048]{2,1,0:T(1,128)S(1)}, u32[]{:S(2)}, u32[]{:S(2)}) async-start(f32[2,1,2048]{2,1,0:T(1,128)} %reshape.119), calls=%async_computation.6 | async-start | bytes 32768 | tf_op jit(solution)/shard_map/all_to_all | solution.py:138
  205.5 3.7 %fusion.99 = bf16[128,16,128]{2,1,0:T(8,128)(2,1)S(1)} fusion(f32[128,128,16]{1,2,0:T(8,128)S(1)} %fusion.14, f32[128,32,128]{2,1,0:T(8,128)} %copy-done.1, f32[128,32,128]{2,1,0:T(8,128)} %copy-done, f32[32,128]{1,0:T(8,128)S(1)} %get-tuple-element.17, f32[32,128]{1,0:T(8,128)S(1)} %get-tuple-element.18), kind=kOutput, calls=%fused_computation.87 | convolution fusion | flops 103029760 | bytes 5799936 | tf_op jit(solution)/shard_map/kn,ckm->cnm/dot_general | solution.py:62
  209.2 0.9 copy.161
  210.2 6.0 %all-to-all-start.2 = ((bf16[128,16,128]{2,0,1:T(8,128)(2,1)}), bf16[128,16,128]{2,0,1:T(8,128)(2,1)S(1)}, u32[]{:S(2)}, u32[]{:S(2)}) async-start(bf16[128,16,128]{2,0,1:T(8,128)(2,1)} %copy.161), calls=%async_computation.2 | async-start | bytes 1048576 | tf_op jit(solution)/shard_map/all_to_all | solution.py:129
  216.2 0.9 copy.172
  217.1 13.3 %all-to-all-done.2 = bf16[128,16,128]{2,0,1:T(8,128)(2,1)S(1)} async-done(((bf16[128,16,128]{2,0,1:T(8,128)(2,1)}), bf16[128,16,128]{2,0,1:T(8,128)(2,1)S(1)}, u32[]{:S(2)}, u32[]{:S(2)}) %all-to-all-start.2) | async-done | bytes 524320 | tf_op jit(solution)/shard_map/all_to_all | solution.py:129
  230.5 4.2 %all-to-all-start.4 = ((bf16[128,16,128]{2,0,1:T(8,128)(2,1)}), bf16[128,16,128]{2,0,1:T(8,128)(2,1)S(1)}, u32[]{:S(2)}, u32[]{:S(2)}) async-start(bf16[128,16,128]{2,0,1:T(8,128)(2,1)} %copy.172), calls=%async_computation.4 | async-start | bytes 1048576 | tf_op jit(solution)/shard_map/all_to_all | solution.py:130
  234.6 0.5 broadcast.243
  235.1 0.7 reduce.3
  235.8 0.7 reshape.120
  236.5 12.4 %all-to-all-done.4 = bf16[128,16,128]{2,0,1:T(8,128)(2,1)S(1)} async-done(((bf16[128,16,128]{2,0,1:T(8,128)(2,1)}), bf16[128,16,128]{2,0,1:T(8,128)(2,1)S(1)}, u32[]{:S(2)}, u32[]{:S(2)}) %all-to-all-start.4) | async-done | bytes 524320 | tf_op jit(solution)/shard_map/all_to_all | solution.py:130
  248.9 0.8 copy.283
  249.7 0.8 copy.284
  (43 shorter events, 2.8 us)
Async XLA Ops:
  0.6 10.9 %copy-start.10 = (f32[64,64]{1,0:T(8,128)S(1)}, f32[64,64]{1,0:T(8,128)}, u32[]{:S(2)}) copy-start(f32[64,64]{1,0:T(8,128)} %param.7) | copy-start | bytes 49156
  4.1 91.5 %all-to-all-start.3 = ((bf16[16,2,8192]{2,1,0:T(2,128)(2,1)}), bf16[16,2,8192]{2,1,0:T(2,128)(2,1)S(1)}, u32[]{:S(2)}, u32[]{:S(2)}) async-start(bf16[16,2,8192]{2,1,0:T(2,128)(2,1)} %reshape.117), calls=%async_computation.3 | async-start | bytes 1048576 | tf_op jit(solution)/shard_map/all_to_all | solution.py:92
  88.5 3.2 %copy-start.8 = (bf16[2048,128]{1,0:T(8,128)(2,1)S(1)}, bf16[2048,128]{1,0:T(8,128)(2,1)}, u32[]{:S(2)}) copy-start(bf16[2048,128]{1,0:T(8,128)(2,1)} %param.5) | copy-start | bytes 1572868
  88.8 4.8 %copy-start.9 = (bf16[2048,128]{1,0:T(8,128)(2,1)S(1)}, bf16[2048,128]{1,0:T(8,128)(2,1)}, u32[]{:S(2)}) copy-start(bf16[2048,128]{1,0:T(8,128)(2,1)} %param.6) | copy-start | bytes 1572868
  95.6 36.4 %all-to-all-start = ((bf16[16,2,8192]{2,1,0:T(2,128)(2,1)}), bf16[16,2,8192]{2,1,0:T(2,128)(2,1)S(1)}, u32[]{:S(2)}, u32[]{:S(2)}) async-start(bf16[16,2,8192]{2,1,0:T(2,128)(2,1)} %reshape.113), calls=%async_computation | async-start | bytes 1048576 | tf_op jit(solution)/shard_map/all_to_all | solution.py:93
  113.6 5.3 %copy-start.3 = (f32[128,32,128]{2,0,1:T(8,128)}, f32[128,32,128]{2,0,1:T(8,128)S(1)}, u32[]{:S(2)}) copy-start(f32[128,32,128]{2,0,1:T(8,128)S(1)} %fusion.63) | copy-start | bytes 6291460
  132.0 20.2 %all-to-all-start.1 = ((bf16[16,2,8192]{2,1,0:T(2,128)(2,1)}), bf16[16,2,8192]{2,1,0:T(2,128)(2,1)S(1)}, u32[]{:S(2)}, u32[]{:S(2)}) async-start(bf16[16,2,8192]{2,1,0:T(2,128)(2,1)} %reshape.115), calls=%async_computation.1 | async-start | bytes 1048576 | tf_op jit(solution)/shard_map/all_to_all | solution.py:96
  138.0 5.1 %copy-start.2 = (f32[128,32,128]{2,1,0:T(8,128)S(1)}, f32[128,32,128]{2,1,0:T(8,128)}, u32[]{:S(2)}) copy-start(f32[128,32,128]{2,1,0:T(8,128)} %fusion.72) | copy-start | bytes 6291460
  147.7 5.5 %copy-start.7 = (bf16[128,16,128]{2,1,0:T(8,128)(2,1)S(1)}, bf16[128,16,128]{2,1,0:T(8,128)(2,1)}, u32[]{:S(2)}) copy-start(bf16[128,16,128]{2,1,0:T(8,128)(2,1)} %fusion.96) | copy-start | bytes 1572868
  168.2 4.0 %copy-start.4 = (f32[128,32,128]{2,0,1:T(8,128)S(1)}, f32[128,32,128]{2,0,1:T(8,128)}, u32[]{:S(2)}) copy-start(f32[128,32,128]{2,0,1:T(8,128)} %copy-done.3) | copy-start | bytes 6291460
  168.3 4.0 %copy-start.6 = (f32[128,32,128]{2,0,1:T(8,128)S(1)}, f32[128,32,128]{2,0,1:T(8,128)}, u32[]{:S(2)}) copy-start(f32[128,32,128]{2,0,1:T(8,128)} %get-tuple-element.15) | copy-start | bytes 6291460
  185.9 15.6 %all-to-all-start.5 = ((f32[2,16,128]{2,0,1:T(2,128)}), f32[2,16,128]{2,0,1:T(2,128)S(1)}, u32[]{:S(2)}, u32[]{:S(2)}) async-start(f32[2,16,128]{2,0,1:T(2,128)} %copy.177), calls=%async_computation.5 | async-start | bytes 32768 | tf_op jit(solution)/shard_map/all_to_all | solution.py:136
  190.0 5.1 %copy-start.5 = (f32[128,32,128]{2,1,0:T(8,128)S(1)}, f32[128,32,128]{2,1,0:T(8,128)}, u32[]{:S(2)}) copy-start(f32[128,32,128]{2,1,0:T(8,128)} %fusion.30) | copy-start | bytes 6291460
  195.2 3.4 %copy-start = (f32[128,32,128]{2,1,0:T(8,128)}, f32[128,32,128]{2,1,0:T(8,128)S(1)}, u32[]{:S(2)}) copy-start(f32[128,32,128]{2,1,0:T(8,128)S(1)} %fusion.66) | copy-start | bytes 6291460
  198.6 1.3 copy-start.1
  202.2 7.9 %all-to-all-start.6 = ((f32[2,1,2048]{2,1,0:T(1,128)}), f32[2,1,2048]{2,1,0:T(1,128)S(1)}, u32[]{:S(2)}, u32[]{:S(2)}) async-start(f32[2,1,2048]{2,1,0:T(1,128)} %reshape.119), calls=%async_computation.6 | async-start | bytes 32768 | tf_op jit(solution)/shard_map/all_to_all | solution.py:138
  210.2 20.3 %all-to-all-start.2 = ((bf16[128,16,128]{2,0,1:T(8,128)(2,1)}), bf16[128,16,128]{2,0,1:T(8,128)(2,1)S(1)}, u32[]{:S(2)}, u32[]{:S(2)}) async-start(bf16[128,16,128]{2,0,1:T(8,128)(2,1)} %copy.161), calls=%async_computation.2 | async-start | bytes 1048576 | tf_op jit(solution)/shard_map/all_to_all | solution.py:129
  230.5 18.4 %all-to-all-start.4 = ((bf16[128,16,128]{2,0,1:T(8,128)(2,1)}), bf16[128,16,128]{2,0,1:T(8,128)(2,1)S(1)}, u32[]{:S(2)}, u32[]{:S(2)}) async-start(bf16[128,16,128]{2,0,1:T(8,128)(2,1)} %copy.172), calls=%async_computation.4 | async-start | bytes 1048576 | tf_op jit(solution)/shard_map/all_to_all | solution.py:130
where the time goes:
time: 255 us; the launch traced here: 251 us
  matrix products  86.2 us (34%)
  blocking collectives  76.8 us (30%)
  starting transfers between devices  34.6 us (14%)
  waiting for transfers between devices  30.3 us (12%)
  local copies, waits for them, and re-layouts  13.3 us (5%)
  other arithmetic  8.07 us (3%)
    all_gather x1, blocking collectives, shards(): whole = lax.all_gather(filters, ('seq', 'chan'), axis=1, tiled=True)  76.8 us
    dot_general x24, matrix products, right_product(): return jnp.einsum('ckm,mj->ckj', values, table, precision=HIGHEST)  71.1 us
    all_to_all x1, waiting for transfers between devices, shards(): lax.all_to_all(grad_input, 'seq', split_axis=1, concat_axis=0, tiled=True)  13.3 us
    all_to_all x1, waiting for transfers between devices, shards(): lax.all_to_all(second, 'seq', split_axis=1, concat_axis=0, tiled=True)  12.4 us
    unnamed x35, local copies, waits for them, and re-layouts  9.53 us
    all_to_all x1, starting transfers between devices, shards(): lax.all_to_all(shaped_inputs, 'seq', split_axis=0, concat_axis=1, tiled=T...  7.39 us
    dot_general x3, matrix products, inverse_dft(): result = jnp.einsum('kn,ckm->cnm', block_cos, real_twist, precision=HIGHEST)  6.22 us
    all_to_all x1, starting transfers between devices, shards(): lax.all_to_all(grad_input, 'seq', split_axis=1, concat_axis=0, tiled=True)  6.01 us
  transfers between devices with their start and end apart: 7, of which 3 were waited for; matrix products, arithmetic and copies ran while one was open for 27% of the time, Pallas kernels for 0%

commit v1 on v0

--- a/solution.py
+++ b/solution.py
@@ -1,8 +1,11 @@
+import functools
 import math
 
 import jax
 import jax.numpy as jnp
 from jax import lax
+from jax.experimental import pallas as pl
+from jax.experimental.pallas import tpu as pltpu
 from jax.sharding import PartitionSpec as P
 
 D = 4096
@@ -139,10 +142,329 @@
     return (returned_input.reshape(chan_rows, block_len), returned_second, grad_filters)
 
 
+GROUP_WIDTH = D // G
+MESH = pl.DeviceIdType.MESH
+TILE = 256
+
+
+def exchange_kernel(
+    seq_count,
+    chan_count,
+    x_ref,
+    gate_ref,
+    up_ref,
+    filt_ref,
+    gi_ref,
+    gg_ref,
+    gf_ref,
+    u_loc,
+    xs,
+    us,
+    ks,
+    cv,
+    gv,
+    acc_c,
+    acc_g,
+    conv_in,
+    fg_out,
+    x_send,
+    x_recv,
+    u_send,
+    u_recv,
+    k_send,
+    k_recv,
+    c_send,
+    c_recv,
+    g_send,
+    g_recv,
+    f_send,
+    f_recv,
+):
+    seq = lax.axis_index("seq")
+    chan = lax.axis_index("chan")
+    everyone = seq_count * chan_count
+    me = seq * chan_count + chan
+    local_groups = xs.shape[0]
+    block = x_ref.shape[1]
+    per_tile = TILE // block
+    length = block * seq_count
+    tiles = length // TILE
+    width = GROUP_WIDTH
+    rows = tiles * width
+    local_chan = local_groups * width
+
+    barrier = pltpu.get_barrier_semaphore()
+
+    def greet(k, carry):
+        other = lax.rem(me + k, everyone)
+        pl.semaphore_signal(
+            barrier,
+            inc=1,
+            device_id=(other // chan_count, lax.rem(other, chan_count)),
+            device_id_type=MESH,
+        )
+        return carry
+
+    lax.fori_loop(1, everyone, greet, 0)
+    pl.semaphore_wait(barrier, everyone - 1)
+
+    def place(ref, g, s):
+        return ref.at[
+            g,
+            pl.ds(pl.multiple_of((s // per_tile) * width, width), width),
+            pl.ds(pl.multiple_of(lax.rem(s, per_tile) * block, block), block),
+        ]
+
+    def strip(ref, s, g):
+        return ref.at[pl.ds(pl.multiple_of(s * local_chan + g * width, width), width), :]
+
+    def forward(ref, buf, send, recv, g, to, slot_from):
+        return pltpu.make_async_remote_copy(
+            src_ref=strip(ref, to, g),
+            dst_ref=place(buf, g, slot_from),
+            send_sem=send.at[g, to],
+            recv_sem=recv.at[g, slot_from],
+            device_id=(to, chan),
+            device_id_type=MESH,
+        )
+
+    def own(ref, buf, recv, g):
+        return pltpu.make_async_copy(strip(ref, seq, g), place(buf, g, seq), recv.at[g, seq])
+
+    def backward(buf, ref, send, recv, g, to, slot_from):
+        return pltpu.make_async_remote_copy(
+            src_ref=place(buf, g, to),
+            dst_ref=strip(ref, slot_from, g),
+            send_sem=send.at[g, to],
+            recv_sem=recv.at[g, slot_from],
+            device_id=(to, chan),
+            device_id_type=MESH,
+        )
+
+    def own_back(buf, ref, recv, g):
+        return pltpu.make_async_copy(place(buf, g, seq), strip(ref, seq, g), recv.at[g, seq])
+
+    def filt_copy(to, slot_from):
+        to_seq, to_chan = to // chan_count, lax.rem(to, chan_count)
+        return pltpu.make_async_remote_copy(
+            src_ref=filt_ref.at[to_chan * seq_count + to_seq],
+            dst_ref=ks.at[slot_from],
+            send_sem=k_send.at[to],
+            recv_sem=k_recv.at[slot_from],
+            device_id=(to_seq, to_chan),
+            device_id_type=MESH,
+        )
+
+    def grad_copy(to, slot_from):
+        to_seq, to_chan = to // chan_count, lax.rem(to, chan_count)
+        from_seq, from_chan = slot_from // chan_count, lax.rem(slot_from, chan_count)
+        return pltpu.make_async_remote_copy(
+            src_ref=fg_out.at[to_seq],
+            dst_ref=gf_ref.at[from_chan * seq_count + from_seq],
+            send_sem=f_send.at[to],
+            recv_sem=f_recv.at[slot_from],
+            device_id=(to_seq, to_chan),
+            device_id_type=MESH,
+        )
+
+    def seq_loop(body):
+        def step(k, carry):
+            body(lax.rem(seq + k, seq_count))
+            return carry
+
+        lax.fori_loop(1, seq_count, step, 0)
+
+    def all_loop(body):
+        def step(k, carry):
+            body(lax.rem(me + k, everyone))
+            return carry
+
+        lax.fori_loop(1, everyone, step, 0)
+
+    all_loop(lambda p: filt_copy(p, me).start())
+    own_filt = pltpu.make_async_copy(
+        filt_ref.at[chan * seq_count + seq], ks.at[me], k_recv.at[me]
+    )
+    own_filt.start()
+    seq_loop(lambda p: forward(x_ref, xs, x_send, x_recv, 0, p, seq).start())
+    own(x_ref, xs, x_recv, 0).start()
+
+    u_loc[...] = (
+        gate_ref[...].astype(jnp.float32) * up_ref[...].astype(jnp.float32)
+    ).astype(jnp.bfloat16)
+    seq_loop(lambda p: forward(u_loc, us, u_send, u_recv, 0, p, seq).start())
+    own(u_loc, us, u_recv, 0).start()
+    for g in range(1, local_groups):
+        seq_loop(lambda p, g=g: forward(x_ref, xs, x_send, x_recv, g, p, seq).start())
+        own(x_ref, xs, x_recv, g).start()
+        seq_loop(lambda p, g=g: forward(u_loc, us, u_send, u_recv, g, p, seq).start())
+        own(u_loc, us, u_recv, g).start()
+
+    for g in range(local_groups):
+        us[g, rows:, :] = jnp.zeros((rows, TILE), jnp.bfloat16)
+    row_id = lax.broadcasted_iota(jnp.int32, (TILE, TILE), 0)
+    col_id = lax.broadcasted_iota(jnp.int32, (TILE, TILE), 1)
+    upper = col_id >= row_id
+    flip = jnp.where(row_id + col_id == TILE - 1, 1.0, 0.0).astype(jnp.bfloat16)
+    lower_flipped = col_id + row_id >= TILE - 1
+    factor = 1.0 / math.sqrt(width * length)
+    nt = (((1,), (1,)), ((), ()))
+    nn = (((1,), (0,)), ((), ()))
+
+    def dot(a, b, dims):
+        return lax.dot_general(a, b, dims, preferred_element_type=jnp.float32)
+
+    all_loop(lambda p: filt_copy(me, p).wait_recv())
+    own_filt.wait()
+
+    def group_step(g, carry):
+        seq_loop(lambda p: forward(x_ref, xs, x_send, x_recv, g, seq, p).wait_recv())
+        own(x_ref, xs, x_recv, g).wait()
+        seq_loop(lambda p: forward(u_loc, us, u_send, u_recv, g, seq, p).wait_recv())
+        own(u_loc, us, u_recv, g).wait()
+        rolled_before = jnp.zeros((TILE, TILE), jnp.float32)
+        for lag in range(tiles):
+            pieces = []
+            for q in range(per_tile):
+                s = lag * per_tile + q
+                part = ks[s * chan_count, pl.ds(g, 1), :]
+                for c in range(1, chan_count):
+                    part = part + ks[s * chan_count + c, pl.ds(g, 1), :]
+                pieces.append(part)
+            row = jnp.concatenate(pieces, axis=1)
+            rolled = pltpu.roll(
+                jnp.broadcast_to(row, (TILE, TILE)), 0, 1, stride=1, stride_axis=0
+            )
+            table = jnp.where(upper, rolled, rolled_before)
+            rolled_before = rolled
+            high = table.astype(jnp.bfloat16)
+            low = (table - high.astype(jnp.float32)).astype(jnp.bfloat16)
+            n = (tiles - lag) * width
+            xin = xs[g, :n, :]
+            uin = us[g, lag * width : rows, :]
+            conv_add = dot(xin, high, nn) + dot(xin, low, nn)
+            grad_add = dot(uin, high, nt) + dot(uin, low, nt)
+            if lag == 0:
+                acc_c[...] = conv_add
+                acc_g[...] = grad_add
+            else:
+                acc_c[lag * width :, :] += conv_add
+                acc_g[:n, :] += grad_add
+        cv[g] = acc_c[...].astype(jnp.bfloat16)
+        gv[g] = acc_g[...].astype(jnp.bfloat16)
+        seq_loop(lambda p: backward(cv, conv_in, c_send, c_recv, g, p, seq).start())
+        own_back(cv, conv_in, c_recv, g).start()
+        seq_loop(lambda p: backward(gv, gi_ref, g_send, g_recv, g, p, seq).start())
+        own_back(gv, gi_ref, g_recv, g).start()
+        turned = dot(flip, xs[g], nt).astype(jnp.bfloat16)
+        gram = dot(turned, us[g, 0:rows, :], nn)
+        for lag in range(tiles):
+            if lag + 1 < tiles:
+                following = dot(turned, us[g, (lag + 1) * width : (lag + 1) * width + rows, :], nn)
+            else:
+                following = jnp.zeros_like(gram)
+            mixed = jnp.where(lower_flipped, gram, following)
+            gram = following
+            aligned = pltpu.roll(mixed, 1, 1, stride=1, stride_axis=0)
+            total = jnp.sum(aligned, axis=0, keepdims=True) * factor
+            for q in range(per_tile):
+                fg_out[lag * per_tile + q, pl.ds(g, 1), :] = total[:, q * block : (q + 1) * block]
+        return carry
+
+    lax.fori_loop(0, local_groups, group_step, 0)
+    all_loop(lambda p: grad_copy(p, me).start())
+    own_grad = pltpu.make_async_copy(
+        fg_out.at[seq], gf_ref.at[chan * seq_count + seq], f_recv.at[me]
+    )
+    own_grad.start()
+
+    for g in range(local_groups):
+        seq_loop(lambda p, g=g: backward(cv, conv_in, c_send, c_recv, g, seq, p).wait_recv())
+        own_back(cv, conv_in, c_recv, g).wait()
+    gg_ref[...] = (up_ref[...].astype(jnp.float32) * conv_in[...].astype(jnp.float32)).astype(
+        jnp.bfloat16
+    )
+    for g in range(local_groups):
+        seq_loop(lambda p, g=g: backward(gv, gi_ref, g_send, g_recv, g, seq, p).wait_recv())
+        own_back(gv, gi_ref, g_recv, g).wait()
+    all_loop(lambda p: grad_copy(me, p).wait_recv())
+    own_grad.wait()
+    for g in range(local_groups):
+        seq_loop(lambda p, g=g: forward(x_ref, xs, x_send, x_recv, g, p, seq).wait_send())
+        seq_loop(lambda p, g=g: forward(u_loc, us, u_send, u_recv, g, p, seq).wait_send())
+        seq_loop(lambda p, g=g: backward(cv, conv_in, c_send, c_recv, g, p, seq).wait_send())
+        seq_loop(lambda p, g=g: backward(gv, gi_ref, g_send, g_recv, g, p, seq).wait_send())
+    all_loop(lambda p: filt_copy(p, me).wait_send())
+    all_loop(lambda p: grad_copy(p, me).wait_send())
+
+
+def fused_shards(inputs, gating, grad_out, filters):
+    seq_count = lax.axis_size("seq")
+    chan_count = lax.axis_size("chan")
+    chan_rows, block = inputs.shape
+    everyone = seq_count * chan_count
+    local_groups = chan_rows // seq_count // GROUP_WIDTH
+    length = block * seq_count
+    share = filters.shape[1]
+    factor = 1.0 / math.sqrt(GROUP_WIDTH * length)
+    chan = lax.axis_index("chan")
+    scaled = (filters * factor).reshape(everyone, local_groups, share)
+    lanes = jnp.tile(scaled, (1, 1, chan_count))
+    held = lax.broadcasted_iota(jnp.int32, lanes.shape, 2) // share == chan
+    packed = jnp.where(held, lanes, 0.0)
+    packed = jnp.pad(packed, ((0, 0), (0, 8 - local_groups), (0, 0)))
+    rows = length // TILE * GROUP_WIDTH
+    vmem = pl.BlockSpec(memory_space=pltpu.VMEM)
+    pair = pltpu.SemaphoreType.DMA((local_groups, seq_count))
+    many = pltpu.SemaphoreType.DMA((everyone,))
+    grad_inputs, grad_gating, grads = pl.pallas_call(
+        functools.partial(exchange_kernel, seq_count, chan_count),
+        out_shape=(
+            jax.ShapeDtypeStruct((chan_rows, block), jnp.bfloat16),
+            jax.ShapeDtypeStruct((chan_rows, block), jnp.bfloat16),
+            jax.ShapeDtypeStruct((everyone, 8, block), jnp.float32),
+        ),
+        in_specs=[vmem] * 4,
+        out_specs=(vmem, vmem, vmem),
+        scratch_shapes=[
+            pltpu.VMEM((chan_rows, block), jnp.bfloat16),
+            pltpu.VMEM((local_groups, rows, TILE), jnp.bfloat16),
+            pltpu.VMEM((local_groups, 2 * rows, TILE), jnp.bfloat16),
+            pltpu.VMEM((everyone, 8, block), jnp.float32),
+            pltpu.VMEM((local_groups, rows, TILE), jnp.bfloat16),
+            pltpu.VMEM((local_groups, rows, TILE), jnp.bfloat16),
+            pltpu.VMEM((rows, TILE), jnp.float32),
+            pltpu.VMEM((rows, TILE), jnp.float32),
+            pltpu.VMEM((chan_rows, block), jnp.bfloat16),
+            pltpu.VMEM((seq_count, 8, block), jnp.float32),
+            pair,
+            pair,
+            pair,
+            pair,
+            many,
+            many,
+            pair,
+            pair,
+            pair,
+            pair,
+            many,
+            many,
+        ],
+        compiler_params=pltpu.CompilerParams(
+            collective_id=0, has_side_effects=True, vmem_limit_bytes=40 * 1024 * 1024
+        ),
+    )(inputs, gating, grad_out, packed)
+    grads = grads[:, :local_groups, :].reshape(G, block)
+    grad_filters = lax.dynamic_slice_in_dim(grads, chan * share, share, 1)
+    return (grad_inputs, grad_gating, grad_filters)
+
+
 def solution(mesh):
     placed = (P("chan", "seq"), P("chan", "seq"), P("chan", "seq"), P(None, ("seq", "chan")))
+    local_chan = D // mesh.shape["chan"] // mesh.shape["seq"]
+    body = fused_shards if local_chan % GROUP_WIDTH == 0 else shards
     return jax.shard_map(
-        shards,
+        body,
         mesh=mesh,
         in_specs=placed,
         out_specs=(P("chan", "seq"), P("chan", "seq"), P(None, ("seq", "chan"))),

time: 255 us -> 71.1 us (0.28); the launches traced: 251 us -> 70.8 us
  matrix products: 86.2 us -> 0 us
  blocking collectives: 76.8 us -> 0 us
  Pallas kernels: 0 us -> 63.7 us
  starting transfers between devices: 34.6 us -> 0 us
  waiting for transfers between devices: 30.3 us -> 0 us
  local copies, waits for them, and re-layouts: 13.3 us -> 5.57 us
  other arithmetic: 8.07 us -> 0.8 us
    dot_general x36 -> x0, matrix products: 86.2 us -> none  [the longest x24 71.1 us: right_product(): return jnp.einsum('ckm,mj->ckj', values, table, precision=HIGHEST)]
    all_gather x1 -> x0, blocking collectives: 76.8 us -> none  [shards(): whole = lax.all_gather(filters, ('seq', 'chan'), axis=1, tiled=True)]
    pallas_call x0 -> x1, Pallas kernels: none -> 63.7 us  [fused_shards(): pl.pallas_call(functools.partial(exchange_kernel, seq_count, chan_count),...]
    all_to_all x7 -> x0, starting transfers between devices: 34.6 us -> none  [the longest x1 7.39 us: shards(): lax.all_to_all(shaped_inputs, 'seq', split_axis=0, concat_axis=1, tiled=T...]
    all_to_all x7 -> x0, waiting for transfers between devices: 30.3 us -> none  [the longest x1 13.3 us: shards(): lax.all_to_all(grad_input, 'seq', split_axis=1, concat_axis=0, tiled=True)]
    unnamed x35 -> x8, local copies, waits for them, and re-layouts: 9.53 us -> 4.7 us
    reshape x3 -> x0, other arithmetic: 4.11 us -> none  [the longest x1 2.06 us: shards(): shaped_inputs = inputs.reshape(chan_rows, 1, block_len)]
  transfers between devices with their start and end apart: 7 -> 0, of which waited for: 3 -> 0; matrix products, arithmetic and copies ran while one was open for 27% -> 0% of each run, Pallas kernels for 0% -> 0%
where the time goes in v1:
time: 71.1 us; the launch traced here: 70.8 us
  Pallas kernels  63.7 us (90%)
  local copies, waits for them, and re-layouts  5.57 us (8%)
  other arithmetic  0.8 us (1%)
    pallas_call x1, Pallas kernels, fused_shards(): pl.pallas_call(functools.partial(exchange_kernel, seq_count, chan_count),...  63.7 us
    unnamed x8, local copies, waits for them, and re-layouts  4.7 us

profile of v1, /device:TPU:0, one launch (start us, length us, event | category | flops | bytes accessed | tf_op | source)
XLA Modules:
  0.0 70.8 jit_solution(17912624424311156629)
XLA Ops:
  0.6 0.8 %broadcast_multiply_fusion = f32[64,64]{1,0:T(8,128)S(1)} fusion(f32[64,64]{1,0:T(8,128)} %param.7), kind=kLoop, calls=%fused_computation.1 | loop fusion | flops 4096 | bytes 32768 | tf_op jit(solution)/shard_map/mul | solution.py:411
  1.4 0.1 tile.12
  1.6 0.0 copy-start
  1.6 1.0 %copy-done = bf16[2048,128]{1,0:T(8,128)(2,1)S(1)} copy-done((bf16[2048,128]{1,0:T(8,128)(2,1)S(1)}, bf16[2048,128]{1,0:T(8,128)(2,1)}, u32[]{:S(2)}) %copy-start) | copy-done | bytes 524312
  2.7 0.0 copy-start.1
  2.7 1.0 %copy-done.1 = bf16[2048,128]{1,0:T(8,128)(2,1)S(1)} copy-done((bf16[2048,128]{1,0:T(8,128)(2,1)S(1)}, bf16[2048,128]{1,0:T(8,128)(2,1)}, u32[]{:S(2)}) %copy-start.1) | copy-done | bytes 524312
  3.7 0.0 copy-start.2
  3.7 1.0 %copy-done.2 = bf16[2048,128]{1,0:T(8,128)(2,1)S(1)} copy-done((bf16[2048,128]{1,0:T(8,128)(2,1)S(1)}, bf16[2048,128]{1,0:T(8,128)(2,1)}, u32[]{:S(2)}) %copy-start.2) | copy-done | bytes 524312
  4.7 63.7 %shard_map.67 = (bf16[2048,128]{1,0:T(8,128)(2,1)S(1)}, bf16[2048,128]{1,0:T(8,128)(2,1)S(1)}, f32[32,8,128]{2,1,0:T(8,128)S(1)}) custom-call(bf16[2048,128]{1,0:T(8,128)(2,1)S(1)} %copy-done, bf16[2048,128]{1,0:T(8,128)(2,1)S(1)} %copy-done.1, bf16[2048,128]{1,0:T(8,128)(2,1)S(1)} %copy-done.2, f32[32,8,128]{2,1,0:T(8,128)S(1)} %pad.4.filt_ref), custom_call_target="tpu_custom_call" | custom-call | tf_op jit(solution)/shard_map/pallas_call | solution.py:420
  68.5 0.7 constant_dynamic-slice_fusion
  69.2 0.8 %copy.9 = bf16[2048,128]{1,0:T(8,128)(2,1)} copy(bf16[2048,128]{1,0:T(8,128)(2,1)S(1)} %get-tuple-element.14) | data formatting | bytes 1048576
  70.0 0.8 %copy.10 = bf16[2048,128]{1,0:T(8,128)(2,1)} copy(bf16[2048,128]{1,0:T(8,128)(2,1)S(1)} %get-tuple-element.15) | data formatting | bytes 1048576
  (6 shorter events, 0.1 us)
Async XLA Ops:
  1.6 1.0 %copy-start = (bf16[2048,128]{1,0:T(8,128)(2,1)S(1)}, bf16[2048,128]{1,0:T(8,128)(2,1)}, u32[]{:S(2)}) copy-start(bf16[2048,128]{1,0:T(8,128)(2,1)} %x_ref.1) | copy-start | bytes 1572868
  2.7 1.0 %copy-start.1 = (bf16[2048,128]{1,0:T(8,128)(2,1)S(1)}, bf16[2048,128]{1,0:T(8,128)(2,1)}, u32[]{:S(2)}) copy-start(bf16[2048,128]{1,0:T(8,128)(2,1)} %gate_ref.1) | copy-start | bytes 1572868
  3.7 1.0 %copy-start.2 = (bf16[2048,128]{1,0:T(8,128)(2,1)S(1)}, bf16[2048,128]{1,0:T(8,128)(2,1)}, u32[]{:S(2)}) copy-start(bf16[2048,128]{1,0:T(8,128)(2,1)} %up_ref.1) | copy-start | bytes 1572868

commit v2 on v1

--- a/solution.py
+++ b/solution.py
@@ -145,9 +145,11 @@
 GROUP_WIDTH = D // G
 MESH = pl.DeviceIdType.MESH
 TILE = 256
-
-
-def exchange_kernel(
+LAYERS = 4
+DELAY_B, DELAY_C, DELAY_D = 1, 2, 4
+
+
+def layered_kernel(
     seq_count,
     chan_count,
     x_ref,
@@ -167,45 +169,73 @@
     acc_g,
     conv_in,
     fg_out,
+    held,
+    part_out,
+    part_in,
     x_send,
     x_recv,
     u_send,
     u_recv,
-    k_send,
-    k_recv,
     c_send,
     c_recv,
     g_send,
     g_recv,
+    z_send,
+    z_recv,
+    p_send,
+    p_recv,
+    k_send,
+    k_recv,
     f_send,
     f_recv,
 ):
     seq = lax.axis_index("seq")
     chan = lax.axis_index("chan")
+    peers = seq_count // LAYERS
+    layer = seq // peers
+    spot = lax.rem(seq, peers)
+    last = LAYERS - 1
     everyone = seq_count * chan_count
     me = seq * chan_count + chan
-    local_groups = xs.shape[0]
+    groups = xs.shape[0]
     block = x_ref.shape[1]
     per_tile = TILE // block
     length = block * seq_count
     tiles = length // TILE
     width = GROUP_WIDTH
     rows = tiles * width
-    local_chan = local_groups * width
+    layer_rows = rows // LAYERS
+    local_chan = groups * width
 
     barrier = pltpu.get_barrier_semaphore()
 
-    def greet(k, carry):
-        other = lax.rem(me + k, everyone)
+    def all_loop(body):
+        def step(k, carry):
+            body(lax.rem(me + k, everyone))
+            return carry
+
+        lax.fori_loop(1, everyone, step, 0)
+
+    def peer_loop(body):
+        for k in range(1, peers):
+            body(lax.rem(spot + k, peers))
+
+    def group_loop(body):
+        def step(g, carry):
+            body(g)
+            return carry
+
+        lax.fori_loop(0, groups, step, 0)
+
+    def greet(p):
         pl.semaphore_signal(
             barrier,
             inc=1,
-            device_id=(other // chan_count, lax.rem(other, chan_count)),
+            device_id=(p // chan_count, lax.rem(p, chan_count)),
             device_id_type=MESH,
         )
-        return carry
-
-    lax.fori_loop(1, everyone, greet, 0)
+
+    all_loop(greet)
     pl.semaphore_wait(barrier, everyone - 1)
 
     def place(ref, g, s):
@@ -215,101 +245,135 @@
             pl.ds(pl.multiple_of(lax.rem(s, per_tile) * block, block), block),
         ]
 
-    def strip(ref, s, g):
-        return ref.at[pl.ds(pl.multiple_of(s * local_chan + g * width, width), width), :]
-
-    def forward(ref, buf, send, recv, g, to, slot_from):
+    def strip(ref, q, g):
+        return ref.at[pl.ds(pl.multiple_of(q * local_chan + g * width, width), width), :]
+
+    def remote(src, dst, send, recv, to_seq, to_chan=None):
         return pltpu.make_async_remote_copy(
-            src_ref=strip(ref, to, g),
-            dst_ref=place(buf, g, slot_from),
-            send_sem=send.at[g, to],
-            recv_sem=recv.at[g, slot_from],
-            device_id=(to, chan),
+            src_ref=src,
+            dst_ref=dst,
+            send_sem=send,
+            recv_sem=recv,
+            device_id=(to_seq, chan if to_chan is None else to_chan),
             device_id_type=MESH,
         )
 
+    def forward(ref, buf, send, recv, g, to, slot):
+        return remote(
+            strip(ref, to, g),
+            place(buf, g, layer * peers + slot),
+            send.at[g, to],
+            recv.at[g, slot],
+            layer * peers + to,
+        )
+
     def own(ref, buf, recv, g):
-        return pltpu.make_async_copy(strip(ref, seq, g), place(buf, g, seq), recv.at[g, seq])
-
-    def backward(buf, ref, send, recv, g, to, slot_from):
-        return pltpu.make_async_remote_copy(
-            src_ref=place(buf, g, to),
-            dst_ref=strip(ref, slot_from, g),
-            send_sem=send.at[g, to],
-            recv_sem=recv.at[g, slot_from],
-            device_id=(to, chan),
-            device_id_type=MESH,
+        return pltpu.make_async_copy(strip(ref, spot, g), place(buf, g, seq), recv.at[g, spot])
+
+    def backward(buf, ref, send, recv, g, to, slot):
+        return remote(
+            place(buf, g, to),
+            strip(ref, slot, g),
+            send.at[g, to],
+            recv.at[g, slot],
+            layer * peers + to,
         )
 
     def own_back(buf, ref, recv, g):
-        return pltpu.make_async_copy(place(buf, g, seq), strip(ref, seq, g), recv.at[g, seq])
-
-    def filt_copy(to, slot_from):
+        return pltpu.make_async_copy(place(buf, g, spot), strip(ref, spot, g), recv.at[g, spot])
+
+    def give_back(buf, ref, send, recv, g):
+        peer_loop(lambda p: backward(buf, ref, send, recv, g, p, spot).start())
+        own_back(buf, ref, recv, g).start()
+
+    def take_back(buf, ref, send, recv, g):
+        peer_loop(lambda p: backward(buf, ref, send, recv, g, spot, p).wait_recv())
+        own_back(buf, ref, recv, g).wait()
+
+    def hop(buf, g, which, step):
+        ref = buf.at[g, pl.ds(which * layer_rows, layer_rows), :]
+        to = jnp.clip(layer + step, 0, last) * peers + spot
+        return remote(ref, ref, z_send.at[g, which], z_recv.at[g, which], to)
+
+    def hand(g, step):
+        to = jnp.clip(layer + step, 0, last) * peers + spot
+        return remote(part_out.at[g], part_in.at[g], p_send.at[g], p_recv.at[g], to)
+
+    def filt_copy(to, slot):
         to_seq, to_chan = to // chan_count, lax.rem(to, chan_count)
-        return pltpu.make_async_remote_copy(
-            src_ref=filt_ref.at[to_chan * seq_count + to_seq],
-            dst_ref=ks.at[slot_from],
-            send_sem=k_send.at[to],
-            recv_sem=k_recv.at[slot_from],
-            device_id=(to_seq, to_chan),
-            device_id_type=MESH,
+        return remote(
+            filt_ref.at[to_chan * peers + lax.rem(to_seq, peers)],
+            ks.at[slot],
+            k_send.at[to],
+            k_recv.at[slot],
+            to_seq,
+            to_chan,
         )
 
-    def grad_copy(to, slot_from):
+    def grad_copy(to, slot):
         to_seq, to_chan = to // chan_count, lax.rem(to, chan_count)
-        from_seq, from_chan = slot_from // chan_count, lax.rem(slot_from, chan_count)
-        return pltpu.make_async_remote_copy(
-            src_ref=fg_out.at[to_seq],
-            dst_ref=gf_ref.at[from_chan * seq_count + from_seq],
-            send_sem=f_send.at[to],
-            recv_sem=f_recv.at[slot_from],
-            device_id=(to_seq, to_chan),
-            device_id_type=MESH,
+        from_seq, from_chan = slot // chan_count, lax.rem(slot, chan_count)
+        return remote(
+            fg_out.at[to_seq],
+            gf_ref.at[from_chan * seq_count + from_seq],
+            f_send.at[to],
+            f_recv.at[slot],
+            to_seq,
+            to_chan,
         )
 
-    def seq_loop(body):
-        def step(k, carry):
-            body(lax.rem(seq + k, seq_count))
-            return carry
-
-        lax.fori_loop(1, seq_count, step, 0)
-
-    def all_loop(body):
-        def step(k, carry):
-            body(lax.rem(me + k, everyone))
-            return carry
-
-        lax.fori_loop(1, everyone, step, 0)
-
-    all_loop(lambda p: filt_copy(p, me).start())
-    own_filt = pltpu.make_async_copy(
-        filt_ref.at[chan * seq_count + seq], ks.at[me], k_recv.at[me]
-    )
-    own_filt.start()
-    seq_loop(lambda p: forward(x_ref, xs, x_send, x_recv, 0, p, seq).start())
-    own(x_ref, xs, x_recv, 0).start()
+    def scatter(ref, buf, send, recv, g):
+        peer_loop(lambda p: forward(ref, buf, send, recv, g, p, spot).start())
+        own(ref, buf, recv, g).start()
 
     u_loc[...] = (
         gate_ref[...].astype(jnp.float32) * up_ref[...].astype(jnp.float32)
     ).astype(jnp.bfloat16)
-    seq_loop(lambda p: forward(u_loc, us, u_send, u_recv, 0, p, seq).start())
-    own(u_loc, us, u_recv, 0).start()
-    for g in range(1, local_groups):
-        seq_loop(lambda p, g=g: forward(x_ref, xs, x_send, x_recv, g, p, seq).start())
-        own(x_ref, xs, x_recv, g).start()
-        seq_loop(lambda p, g=g: forward(u_loc, us, u_send, u_recv, g, p, seq).start())
-        own(u_loc, us, u_recv, g).start()
-
-    for g in range(local_groups):
-        us[g, rows:, :] = jnp.zeros((rows, TILE), jnp.bfloat16)
+
+    def scatter_both(g):
+        scatter(x_ref, xs, x_send, x_recv, g)
+        scatter(u_loc, us, u_send, u_recv, g)
+
+    scatter_both(0)
+    all_loop(lambda p: filt_copy(p, me).start())
+    own_filt = pltpu.make_async_copy(filt_ref.at[chan * peers + spot], ks.at[me], k_recv.at[me])
+    own_filt.start()
+
+    def scatter_rest(g):
+        @pl.when(g > 0)
+        def _():
+            scatter_both(g)
+
+    group_loop(scatter_rest)
+
+    for which in range(LAYERS):
+        span = slice(which * layer_rows, (which + 1) * layer_rows)
+        empty = jnp.zeros((groups, layer_rows, TILE), jnp.bfloat16)
+        has_x = (layer == which) | ((layer > which) & (layer < last))
+        has_u = (layer == which) | ((layer < which) & (layer > 0))
+
+        @pl.when(jnp.logical_not(has_x))
+        def _():
+            xs[:, span, :] = empty
+
+        @pl.when(jnp.logical_not(has_u))
+        def _():
+            us[:, span, :] = empty
+
+    us[:, rows:, :] = jnp.zeros((groups, rows, TILE), jnp.bfloat16)
     row_id = lax.broadcasted_iota(jnp.int32, (TILE, TILE), 0)
     col_id = lax.broadcasted_iota(jnp.int32, (TILE, TILE), 1)
     upper = col_id >= row_id
     flip = jnp.where(row_id + col_id == TILE - 1, 1.0, 0.0).astype(jnp.bfloat16)
     lower_flipped = col_id + row_id >= TILE - 1
+    columns = lax.broadcasted_iota(jnp.int32, (TILE, rows), 1)
+    first = jnp.where(layer == 2, 2 * layer_rows, 0)
+    end = jnp.where(layer == 2, 3 * layer_rows, rows)
+    counted = (columns >= first) & (columns < end)
     factor = 1.0 / math.sqrt(width * length)
     nt = (((1,), (1,)), ((), ()))
     nn = (((1,), (0,)), ((), ()))
+    mine = pl.ds(pl.multiple_of(layer * layer_rows, layer_rows), layer_rows)
 
     def dot(a, b, dims):
         return lax.dot_general(a, b, dims, preferred_element_type=jnp.float32)
@@ -317,11 +381,45 @@
     all_loop(lambda p: filt_copy(me, p).wait_recv())
     own_filt.wait()
 
-    def group_step(g, carry):
-        seq_loop(lambda p: forward(x_ref, xs, x_send, x_recv, g, seq, p).wait_recv())
+    def gather_layer(g):
+        peer_loop(lambda p: forward(x_ref, xs, x_send, x_recv, g, spot, p).wait_recv())
         own(x_ref, xs, x_recv, g).wait()
-        seq_loop(lambda p: forward(u_loc, us, u_send, u_recv, g, seq, p).wait_recv())
+        peer_loop(lambda p: forward(u_loc, us, u_send, u_recv, g, spot, p).wait_recv())
         own(u_loc, us, u_recv, g).wait()
+        for which in (0, 1):
+
+            @pl.when(layer == which)
+            def _():
+                hop(xs, g, which, 1).start()
+
+        for which in (2, 3):
+
+            @pl.when(layer == which)
+            def _():
+                hop(us, g, which, -1).start()
+
+    def relay(g):
+        @pl.when(layer == 1)
+        def _():
+            hop(xs, g, 0, 1).wait_recv()
+            hop(xs, g, 0, 1).start()
+
+        @pl.when(layer == 2)
+        def _():
+            hop(us, g, 3, -1).wait_recv()
+            hop(us, g, 3, -1).start()
+
+    def compute(g):
+        @pl.when(layer == 1)
+        def _():
+            hop(us, g, 2, -1).wait_recv()
+            hop(us, g, 3, -1).wait_recv()
+
+        @pl.when(layer == 2)
+        def _():
+            hop(xs, g, 1, 1).wait_recv()
+            hop(xs, g, 0, 1).wait_recv()
+
         rolled_before = jnp.zeros((TILE, TILE), jnp.float32)
         for lag in range(tiles):
             pieces = []
@@ -350,17 +448,41 @@
             else:
                 acc_c[lag * width :, :] += conv_add
                 acc_g[:n, :] += grad_add
-        cv[g] = acc_c[...].astype(jnp.bfloat16)
-        gv[g] = acc_g[...].astype(jnp.bfloat16)
-        seq_loop(lambda p: backward(cv, conv_in, c_send, c_recv, g, p, seq).start())
-        own_back(cv, conv_in, c_recv, g).start()
-        seq_loop(lambda p: backward(gv, gi_ref, g_send, g_recv, g, p, seq).start())
-        own_back(gv, gi_ref, g_recv, g).start()
-        turned = dot(flip, xs[g], nt).astype(jnp.bfloat16)
+
+        @pl.when(layer == 2)
+        def _():
+            part_out[g] = acc_c[last * layer_rows :, :]
+            hand(g, 1).start()
+
+        @pl.when(layer == 1)
+        def _():
+            part_out[g] = acc_g[:layer_rows, :]
+            hand(g, -1).start()
+
+        @pl.when(layer < last)
+        def _():
+            cv[g] = acc_c[mine, :].astype(jnp.bfloat16)
+            give_back(cv, conv_in, c_send, c_recv, g)
+
+        @pl.when(layer == last)
+        def _():
+            held[g] = acc_c[mine, :]
+
+        @pl.when(layer > 0)
+        def _():
+            gv[g] = acc_g[mine, :].astype(jnp.bfloat16)
+            give_back(gv, gi_ref, g_send, g_recv, g)
+
+        @pl.when(layer == 0)
+        def _():
+            held[g] = acc_g[mine, :]
+
+        turned = jnp.where(counted, dot(flip, xs[g], nt), 0.0).astype(jnp.bfloat16)
         gram = dot(turned, us[g, 0:rows, :], nn)
         for lag in range(tiles):
             if lag + 1 < tiles:
-                following = dot(turned, us[g, (lag + 1) * width : (lag + 1) * width + rows, :], nn)
+                start = (lag + 1) * width
+                following = dot(turned, us[g, start : start + rows, :], nn)
             else:
                 following = jnp.zeros_like(gram)
             mixed = jnp.where(lower_flipped, gram, following)
@@ -369,102 +491,144 @@
             total = jnp.sum(aligned, axis=0, keepdims=True) * factor
             for q in range(per_tile):
                 fg_out[lag * per_tile + q, pl.ds(g, 1), :] = total[:, q * block : (q + 1) * block]
+
+    def finish(g):
+        @pl.when(layer == last)
+        def _():
+            hand(g, 1).wait_recv()
+            cv[g] = (held[g] + part_in[g]).astype(jnp.bfloat16)
+            give_back(cv, conv_in, c_send, c_recv, g)
+
+        @pl.when(layer == 0)
+        def _():
+            hand(g, -1).wait_recv()
+            gv[g] = (held[g] + part_in[g]).astype(jnp.bfloat16)
+            give_back(gv, gi_ref, g_send, g_recv, g)
+
+    def stage(step, delay, body):
+        @pl.when((step >= delay) & (step < groups + delay))
+        def _():
+            body(step - delay)
+
+    def pipeline(step, carry):
+        stage(step, 0, gather_layer)
+        stage(step, DELAY_B, relay)
+        stage(step, DELAY_C, compute)
+        stage(step, DELAY_D, finish)
         return carry
 
-    lax.fori_loop(0, local_groups, group_step, 0)
+    lax.fori_loop(0, groups + DELAY_C, pipeline, 0)
     all_loop(lambda p: grad_copy(p, me).start())
     own_grad = pltpu.make_async_copy(
         fg_out.at[seq], gf_ref.at[chan * seq_count + seq], f_recv.at[me]
     )
     own_grad.start()
-
-    for g in range(local_groups):
-        seq_loop(lambda p, g=g: backward(cv, conv_in, c_send, c_recv, g, seq, p).wait_recv())
-        own_back(cv, conv_in, c_recv, g).wait()
+    for g in range(groups + DELAY_C - DELAY_D, groups):
+        finish(g)
+
+    group_loop(lambda g: take_back(cv, conv_in, c_send, c_recv, g))
     gg_ref[...] = (up_ref[...].astype(jnp.float32) * conv_in[...].astype(jnp.float32)).astype(
         jnp.bfloat16
     )
-    for g in range(local_groups):
-        seq_loop(lambda p, g=g: backward(gv, gi_ref, g_send, g_recv, g, seq, p).wait_recv())
-        own_back(gv, gi_ref, g_recv, g).wait()
+    group_loop(lambda g: take_back(gv, gi_ref, g_send, g_recv, g))
     all_loop(lambda p: grad_copy(me, p).wait_recv())
     own_grad.wait()
-    for g in range(local_groups):
-        seq_loop(lambda p, g=g: forward(x_ref, xs, x_send, x_recv, g, p, seq).wait_send())
-        seq_loop(lambda p, g=g: forward(u_loc, us, u_send, u_recv, g, p, seq).wait_send())
-        seq_loop(lambda p, g=g: backward(cv, conv_in, c_send, c_recv, g, p, seq).wait_send())
-        seq_loop(lambda p, g=g: backward(gv, gi_ref, g_send, g_recv, g, p, seq).wait_send())
+
+    def drain(g):
+        peer_loop(lambda p: forward(x_ref, xs, x_send, x_recv, g, p, spot).wait_send())
+        peer_loop(lambda p: forward(u_loc, us, u_send, u_recv, g, p, spot).wait_send())
+        peer_loop(lambda p: backward(cv, conv_in, c_send, c_recv, g, p, spot).wait_send())
+        peer_loop(lambda p: backward(gv, gi_ref, g_send, g_recv, g, p, spot).wait_send())
+
+        @pl.when(layer == 0)
+        def _():
+            hop(xs, g, 0, 1).wait_send()
+
+        @pl.when(layer == 1)
+        def _():
+            hop(xs, g, 0, 1).wait_send()
+            hop(xs, g, 1, 1).wait_send()
+            hand(g, -1).wait_send()
+
+        @pl.when(layer == 2)
+        def _():
+            hop(us, g, 2, -1).wait_send()
+            hop(us, g, 3, -1).wait_send()
+            hand(g, 1).wait_send()
+
+        @pl.when(layer == 3)
+        def _():
+            hop(us, g, 3, -1).wait_send()
+
+    group_loop(drain)
     all_loop(lambda p: filt_copy(p, me).wait_send())
     all_loop(lambda p: grad_copy(p, me).wait_send())
 
 
-def fused_shards(inputs, gating, grad_out, filters):
+def layered_shards(inputs, gating, grad_out, filters):
     seq_count = lax.axis_size("seq")
     chan_count = lax.axis_size("chan")
     chan_rows, block = inputs.shape
     everyone = seq_count * chan_count
-    local_groups = chan_rows // seq_count // GROUP_WIDTH
+    peers = seq_count // LAYERS
+    groups = chan_rows // peers // GROUP_WIDTH
     length = block * seq_count
     share = filters.shape[1]
     factor = 1.0 / math.sqrt(GROUP_WIDTH * length)
     chan = lax.axis_index("chan")
-    scaled = (filters * factor).reshape(everyone, local_groups, share)
-    lanes = jnp.tile(scaled, (1, 1, chan_count))
-    held = lax.broadcasted_iota(jnp.int32, lanes.shape, 2) // share == chan
-    packed = jnp.where(held, lanes, 0.0)
-    packed = jnp.pad(packed, ((0, 0), (0, 8 - local_groups), (0, 0)))
+    lanes = jnp.tile(filters * factor, (1, chan_count))
+    kept = lax.broadcasted_iota(jnp.int32, lanes.shape, 1) // share == chan
+    packed = jnp.where(kept, lanes, 0.0).reshape(chan_count * peers, groups, block)
     rows = length // TILE * GROUP_WIDTH
+    layer_rows = rows // LAYERS
     vmem = pl.BlockSpec(memory_space=pltpu.VMEM)
-    pair = pltpu.SemaphoreType.DMA((local_groups, seq_count))
+    pair = pltpu.SemaphoreType.DMA((groups, peers))
+    stacked = pltpu.SemaphoreType.DMA((groups, LAYERS))
+    single = pltpu.SemaphoreType.DMA((groups,))
     many = pltpu.SemaphoreType.DMA((everyone,))
     grad_inputs, grad_gating, grads = pl.pallas_call(
-        functools.partial(exchange_kernel, seq_count, chan_count),
+        functools.partial(layered_kernel, seq_count, chan_count),
         out_shape=(
             jax.ShapeDtypeStruct((chan_rows, block), jnp.bfloat16),
             jax.ShapeDtypeStruct((chan_rows, block), jnp.bfloat16),
-            jax.ShapeDtypeStruct((everyone, 8, block), jnp.float32),
+            jax.ShapeDtypeStruct((everyone, groups, block), jnp.float32),
         ),
         in_specs=[vmem] * 4,
         out_specs=(vmem, vmem, vmem),
         scratch_shapes=[
             pltpu.VMEM((chan_rows, block), jnp.bfloat16),
-            pltpu.VMEM((local_groups, rows, TILE), jnp.bfloat16),
-            pltpu.VMEM((local_groups, 2 * rows, TILE), jnp.bfloat16),
-            pltpu.VMEM((everyone, 8, block), jnp.float32),
-            pltpu.VMEM((local_groups, rows, TILE), jnp.bfloat16),
-            pltpu.VMEM((local_groups, rows, TILE), jnp.bfloat16),
+            pltpu.VMEM((groups, rows, TILE), jnp.bfloat16),
+            pltpu.VMEM((groups, 2 * rows, TILE), jnp.bfloat16),
+            pltpu.VMEM((everyone, groups, block), jnp.float32),
+            pltpu.VMEM((groups, layer_rows, TILE), jnp.bfloat16),
+            pltpu.VMEM((groups, layer_rows, TILE), jnp.bfloat16),
             pltpu.VMEM((rows, TILE), jnp.float32),
             pltpu.VMEM((rows, TILE), jnp.float32),
             pltpu.VMEM((chan_rows, block), jnp.bfloat16),
-            pltpu.VMEM((seq_count, 8, block), jnp.float32),
-            pair,
-            pair,
-            pair,
-            pair,
-            many,
-            many,
-            pair,
-            pair,
-            pair,
-            pair,
-            many,
-            many,
-        ],
+            pltpu.VMEM((seq_count, groups, block), jnp.float32),
+            pltpu.VMEM((groups, layer_rows, TILE), jnp.float32),
+            pltpu.VMEM((groups, layer_rows, TILE), jnp.float32),
+            pltpu.VMEM((groups, layer_rows, TILE), jnp.float32),
+        ]
+        + [pair] * 8
+        + [stacked] * 2
+        + [single] * 2
+        + [many] * 4,
         compiler_params=pltpu.CompilerParams(
             collective_id=0, has_side_effects=True, vmem_limit_bytes=40 * 1024 * 1024
         ),
     )(inputs, gating, grad_out, packed)
-    grads = grads[:, :local_groups, :].reshape(G, block)
+    grads = grads.reshape(chan_count, LAYERS, peers * groups, block).sum(axis=1)
+    grads = grads.reshape(G, block)
     grad_filters = lax.dynamic_slice_in_dim(grads, chan * share, share, 1)
     return (grad_inputs, grad_gating, grad_filters)
 
 
 def solution(mesh):
     placed = (P("chan", "seq"), P("chan", "seq"), P("chan", "seq"), P(None, ("seq", "chan")))
-    local_chan = D // mesh.shape["chan"] // mesh.shape["seq"]
-    body = fused_shards if local_chan % GROUP_WIDTH == 0 else shards
+    layered = mesh.shape["seq"] == 16 and mesh.shape["chan"] == 2
     return jax.shard_map(
-        body,
+        layered_shards if layered else shards,
         mesh=mesh,
         in_specs=placed,
         out_specs=(P("chan", "seq"), P("chan", "seq"), P(None, ("seq", "chan"))),

time: 71.1 us -> 67 us (0.942)
  Pallas kernels: 63.7 us -> 59.6 us
    pallas_call x1, Pallas kernels: 63.7 us -> 59.6 us  [layered_shards(): pl.pallas_call(functools.partial(layered_kernel, seq_count, chan_count),...]
where the time goes in v2:
time: 67 us; the launch traced here: 66.6 us
  Pallas kernels  59.6 us (89%)
  local copies, waits for them, and re-layouts  5.53 us (8%)
  other arithmetic  0.8 us (1%)
  between operations  0.67 us (1%)
    pallas_call x1, Pallas kernels, layered_shards(): pl.pallas_call(functools.partial(layered_kernel, seq_count, chan_count),...  59.6 us
    unnamed x8, local copies, waits for them, and re-layouts  4.7 us

profile of v2, /device:TPU:0, one launch (start us, length us, event | category | flops | bytes accessed | tf_op | source)
XLA Modules:
  0.0 66.6 jit_solution(9295993559658201758)
XLA Ops:
  0.6 0.8 %broadcast_multiply_fusion = f32[64,64]{1,0:T(8,128)S(1)} fusion(f32[64,64]{1,0:T(8,128)} %param.7), kind=kLoop, calls=%fused_computation.2 | loop fusion | flops 4096 | bytes 32768 | tf_op jit(solution)/shard_map/mul | solution.py:579
  1.4 0.1 tile.10
  1.6 0.0 copy-start
  1.6 1.0 %copy-done = bf16[2048,128]{1,0:T(8,128)(2,1)S(1)} copy-done((bf16[2048,128]{1,0:T(8,128)(2,1)S(1)}, bf16[2048,128]{1,0:T(8,128)(2,1)}, u32[]{:S(2)}) %copy-start) | copy-done | bytes 524312
  2.6 0.0 copy-start.1
  2.6 1.0 %copy-done.1 = bf16[2048,128]{1,0:T(8,128)(2,1)S(1)} copy-done((bf16[2048,128]{1,0:T(8,128)(2,1)S(1)}, bf16[2048,128]{1,0:T(8,128)(2,1)}, u32[]{:S(2)}) %copy-start.1) | copy-done | bytes 524312
  3.6 0.0 copy-start.2
  3.6 1.0 %copy-done.2 = bf16[2048,128]{1,0:T(8,128)(2,1)S(1)} copy-done((bf16[2048,128]{1,0:T(8,128)(2,1)S(1)}, bf16[2048,128]{1,0:T(8,128)(2,1)}, u32[]{:S(2)}) %copy-start.2) | copy-done | bytes 524312
  4.7 59.6 %shard_map.67 = (bf16[2048,128]{1,0:T(8,128)(2,1)S(1)}, bf16[2048,128]{1,0:T(8,128)(2,1)S(1)}, f32[32,8,128]{2,1,0:T(8,128)S(1)}) custom-call(bf16[2048,128]{1,0:T(8,128)(2,1)S(1)} %copy-done, bf16[2048,128]{1,0:T(8,128)(2,1)S(1)} %copy-done.1, bf16[2048,128]{1,0:T(8,128)(2,1)S(1)} %copy-done.2, f32[8,8,128]{2,1,0:T(8,128)S(1)} %fusion.filt_ref), custom_call_target="tpu_custom_call" | custom-call | tf_op jit(solution)/shard_map/pallas_call | solution.py:589
  64.3 0.7 %constant_dynamic-slice_fusion = f32[64,64]{1,0:T(8,128)} fusion(f32[64,128]{1,0:T(8,128)S(1)} %bitcast.3, s32[]{:T(128)S(6)} %select_n.16), kind=kLoop, calls=%fused_computation.8 | loop fusion | bytes 32772 | tf_op jit(solution)/shard_map/dynamic_slice | solution.py:623
  65.0 0.8 %copy.9 = bf16[2048,128]{1,0:T(8,128)(2,1)} copy(bf16[2048,128]{1,0:T(8,128)(2,1)S(1)} %get-tuple-element.14) | data formatting | bytes 1048576
  65.8 0.8 %copy.10 = bf16[2048,128]{1,0:T(8,128)(2,1)} copy(bf16[2048,128]{1,0:T(8,128)(2,1)S(1)} %get-tuple-element.15) | data formatting | bytes 1048576
  (5 shorter events, 0.1 us)
Async XLA Ops:
  1.6 1.0 %copy-start = (bf16[2048,128]{1,0:T(8,128)(2,1)S(1)}, bf16[2048,128]{1,0:T(8,128)(2,1)}, u32[]{:S(2)}) copy-start(bf16[2048,128]{1,0:T(8,128)(2,1)} %x_ref.1) | copy-start | bytes 1572868
  2.6 1.0 %copy-start.1 = (bf16[2048,128]{1,0:T(8,128)(2,1)S(1)}, bf16[2048,128]{1,0:T(8,128)(2,1)}, u32[]{:S(2)}) copy-start(bf16[2048,128]{1,0:T(8,128)(2,1)} %gate_ref.1) | copy-start | bytes 1572868
  3.6 1.0 %copy-start.2 = (bf16[2048,128]{1,0:T(8,128)(2,1)S(1)}, bf16[2048,128]{1,0:T(8,128)(2,1)}, u32[]{:S(2)}) copy-start(bf16[2048,128]{1,0:T(8,128)(2,1)} %up_ref.1) | copy-start | bytes 1572868

commit v3 on v2

--- a/solution.py
+++ b/solution.py
@@ -153,11 +153,15 @@
     seq_count,
     chan_count,
     x_ref,
+    gate_hbm,
+    up_hbm,
+    raw_ref,
+    gi_ref,
+    gg_ref,
+    grad_ref,
     gate_ref,
     up_ref,
     filt_ref,
-    gi_ref,
-    gg_ref,
     gf_ref,
     u_loc,
     xs,
@@ -188,6 +192,7 @@
     k_recv,
     f_send,
     f_recv,
+    in_sem,
 ):
     seq = lax.axis_index("seq")
     chan = lax.axis_index("chan")
@@ -235,7 +240,25 @@
             device_id_type=MESH,
         )
 
+    gate_in = pltpu.make_async_copy(gate_hbm, gate_ref, in_sem.at[0])
+    up_in = pltpu.make_async_copy(up_hbm, up_ref, in_sem.at[1])
+    gate_in.start()
+    up_in.start()
     all_loop(greet)
+    share = raw_ref.shape[1]
+    factor = 1.0 / math.sqrt(width * length)
+    scaled = raw_ref[...] * factor
+    lanes = jnp.concatenate([scaled] * chan_count, axis=1)
+    kept = lax.broadcasted_iota(jnp.int32, lanes.shape, 1) // share == chan
+    lanes = jnp.where(kept, lanes, 0.0)
+    for i in range(chan_count * peers):
+        filt_ref[i] = lanes[i * groups : (i + 1) * groups, :]
+    gate_in.wait()
+    up_in.wait()
+    u_loc[...] = (
+        gate_ref[...].astype(jnp.float32) * up_ref[...].astype(jnp.float32)
+    ).astype(jnp.bfloat16)
+    fg_out[...] = jnp.zeros_like(fg_out)
     pl.semaphore_wait(barrier, everyone - 1)
 
     def place(ref, g, s):
@@ -326,10 +349,6 @@
         peer_loop(lambda p: forward(ref, buf, send, recv, g, p, spot).start())
         own(ref, buf, recv, g).start()
 
-    u_loc[...] = (
-        gate_ref[...].astype(jnp.float32) * up_ref[...].astype(jnp.float32)
-    ).astype(jnp.bfloat16)
-
     def scatter_both(g):
         scatter(x_ref, xs, x_send, x_recv, g)
         scatter(u_loc, us, u_send, u_recv, g)
@@ -349,12 +368,7 @@
     for which in range(LAYERS):
         span = slice(which * layer_rows, (which + 1) * layer_rows)
         empty = jnp.zeros((groups, layer_rows, TILE), jnp.bfloat16)
-        has_x = (layer == which) | ((layer > which) & (layer < last))
         has_u = (layer == which) | ((layer < which) & (layer > 0))
-
-        @pl.when(jnp.logical_not(has_x))
-        def _():
-            xs[:, span, :] = empty
 
         @pl.when(jnp.logical_not(has_u))
         def _():
@@ -366,20 +380,12 @@
     upper = col_id >= row_id
     flip = jnp.where(row_id + col_id == TILE - 1, 1.0, 0.0).astype(jnp.bfloat16)
     lower_flipped = col_id + row_id >= TILE - 1
-    columns = lax.broadcasted_iota(jnp.int32, (TILE, rows), 1)
-    first = jnp.where(layer == 2, 2 * layer_rows, 0)
-    end = jnp.where(layer == 2, 3 * layer_rows, rows)
-    counted = (columns >= first) & (columns < end)
-    factor = 1.0 / math.sqrt(width * length)
     nt = (((1,), (1,)), ((), ()))
     nn = (((1,), (0,)), ((), ()))
-    mine = pl.ds(pl.multiple_of(layer * layer_rows, layer_rows), layer_rows)
+    half = tiles // LAYERS
 
     def dot(a, b, dims):
         return lax.dot_general(a, b, dims, preferred_element_type=jnp.float32)
-
-    all_loop(lambda p: filt_copy(me, p).wait_recv())
-    own_filt.wait()
 
     def gather_layer(g):
         peer_loop(lambda p: forward(x_ref, xs, x_send, x_recv, g, spot, p).wait_recv())
@@ -410,18 +416,46 @@
             hop(us, g, 3, -1).start()
 
     def compute(g):
-        @pl.when(layer == 1)
-        def _():
+        @pl.when(g == 0)
+        def _():
+            all_loop(lambda p: filt_copy(me, p).wait_recv())
+            own_filt.wait()
+
+        for which in range(LAYERS):
+
+            @pl.when(layer == which)
+            def _(which=which):
+                compute_for(which, g)
+
+    def compute_for(which, g):
+        low_end, high_end = which * half, (which + 1) * half - 1
+        x_first = low_end if which == last else 0
+        u_last = high_end if which == 0 else tiles - 1
+        conv_last = tiles - 1 if which == 2 else high_end
+        grad_first = 0 if which == 1 else low_end
+        gram_first = 0 if which == 1 else low_end
+        if which == 1:
             hop(us, g, 2, -1).wait_recv()
             hop(us, g, 3, -1).wait_recv()
-
-        @pl.when(layer == 2)
-        def _():
+        if which == 2:
             hop(xs, g, 1, 1).wait_recv()
             hop(xs, g, 0, 1).wait_recv()
 
+        def span(first, final):
+            return slice(first * width, (final + 1) * width)
+
+        acc_c[span(low_end, conv_last), :] = jnp.zeros(
+            ((conv_last - low_end + 1) * width, TILE), jnp.float32
+        )
+        acc_g[span(grad_first, high_end), :] = jnp.zeros(
+            ((high_end - grad_first + 1) * width, TILE), jnp.float32
+        )
         rolled_before = jnp.zeros((TILE, TILE), jnp.float32)
         for lag in range(tiles):
+            first, final = max(x_first, low_end - lag), min(high_end, conv_last - lag)
+            u_from, u_to = max(low_end, grad_first + lag), min(u_last, high_end + lag)
+            if first > final and u_from > u_to:
+                break
             pieces = []
             for q in range(per_tile):
                 s = lag * per_tile + q
@@ -437,54 +471,43 @@
             rolled_before = rolled
             high = table.astype(jnp.bfloat16)
             low = (table - high.astype(jnp.float32)).astype(jnp.bfloat16)
-            n = (tiles - lag) * width
-            xin = xs[g, :n, :]
-            uin = us[g, lag * width : rows, :]
-            conv_add = dot(xin, high, nn) + dot(xin, low, nn)
-            grad_add = dot(uin, high, nt) + dot(uin, low, nt)
-            if lag == 0:
-                acc_c[...] = conv_add
-                acc_g[...] = grad_add
-            else:
-                acc_c[lag * width :, :] += conv_add
-                acc_g[:n, :] += grad_add
-
-        @pl.when(layer == 2)
-        def _():
+            if first <= final:
+                xin = xs[g, span(first, final), :]
+                acc_c[span(first + lag, final + lag), :] += dot(xin, high, nn) + dot(xin, low, nn)
+            if u_from <= u_to:
+                uin = us[g, span(u_from, u_to), :]
+                acc_g[span(u_from - lag, u_to - lag), :] += dot(uin, high, nt) + dot(uin, low, nt)
+
+        mine = span(low_end, high_end)
+        if which == 2:
             part_out[g] = acc_c[last * layer_rows :, :]
             hand(g, 1).start()
-
-        @pl.when(layer == 1)
-        def _():
+        if which == 1:
             part_out[g] = acc_g[:layer_rows, :]
             hand(g, -1).start()
-
-        @pl.when(layer < last)
-        def _():
+        if which < last:
             cv[g] = acc_c[mine, :].astype(jnp.bfloat16)
             give_back(cv, conv_in, c_send, c_recv, g)
-
-        @pl.when(layer == last)
-        def _():
+        else:
             held[g] = acc_c[mine, :]
-
-        @pl.when(layer > 0)
-        def _():
+        if which > 0:
             gv[g] = acc_g[mine, :].astype(jnp.bfloat16)
             give_back(gv, gi_ref, g_send, g_recv, g)
-
-        @pl.when(layer == 0)
-        def _():
+        else:
             held[g] = acc_g[mine, :]
 
-        turned = jnp.where(counted, dot(flip, xs[g], nt), 0.0).astype(jnp.bfloat16)
-        gram = dot(turned, us[g, 0:rows, :], nn)
-        for lag in range(tiles):
-            if lag + 1 < tiles:
-                start = (lag + 1) * width
-                following = dot(turned, us[g, start : start + rows, :], nn)
-            else:
-                following = jnp.zeros_like(gram)
+        x_span = span(gram_first, high_end)
+        x_rows = (high_end - gram_first + 1) * width
+        turned = dot(flip, xs[g, x_span, :], nt).astype(jnp.bfloat16)
+
+        def gram_of(lag):
+            start = (gram_first + lag) * width
+            return dot(turned, us[g, start : start + x_rows, :], nn)
+
+        gram = gram_of(0)
+        final_lag = u_last - gram_first
+        for lag in range(final_lag + 1):
+            following = gram_of(lag + 1) if lag < final_lag else jnp.zeros_like(gram)
             mixed = jnp.where(lower_flipped, gram, following)
             gram = following
             aligned = pltpu.roll(mixed, 1, 1, stride=1, stride_axis=0)
@@ -533,6 +556,16 @@
     group_loop(lambda g: take_back(gv, gi_ref, g_send, g_recv, g))
     all_loop(lambda p: grad_copy(me, p).wait_recv())
     own_grad.wait()
+    for c in range(chan_count):
+        for q in range(peers):
+            total = gf_ref[c * seq_count + q]
+            for which in range(1, LAYERS):
+                total = total + gf_ref[c * seq_count + which * peers + q]
+            kept_part = total[:, :share]
+            for d in range(1, chan_count):
+                kept_part = jnp.where(chan == d, total[:, d * share : (d + 1) * share], kept_part)
+            at = (c * peers + q) * groups
+            grad_ref[at : at + groups, :] = kept_part
 
     def drain(g):
         peer_loop(lambda p: forward(x_ref, xs, x_send, x_recv, g, p, spot).wait_send())
@@ -573,29 +606,28 @@
     peers = seq_count // LAYERS
     groups = chan_rows // peers // GROUP_WIDTH
     length = block * seq_count
-    share = filters.shape[1]
-    factor = 1.0 / math.sqrt(GROUP_WIDTH * length)
-    chan = lax.axis_index("chan")
-    lanes = jnp.tile(filters * factor, (1, chan_count))
-    kept = lax.broadcasted_iota(jnp.int32, lanes.shape, 1) // share == chan
-    packed = jnp.where(kept, lanes, 0.0).reshape(chan_count * peers, groups, block)
     rows = length // TILE * GROUP_WIDTH
     layer_rows = rows // LAYERS
     vmem = pl.BlockSpec(memory_space=pltpu.VMEM)
+    hbm = pl.BlockSpec(memory_space=pltpu.HBM)
     pair = pltpu.SemaphoreType.DMA((groups, peers))
     stacked = pltpu.SemaphoreType.DMA((groups, LAYERS))
     single = pltpu.SemaphoreType.DMA((groups,))
     many = pltpu.SemaphoreType.DMA((everyone,))
-    grad_inputs, grad_gating, grads = pl.pallas_call(
+    return pl.pallas_call(
         functools.partial(layered_kernel, seq_count, chan_count),
         out_shape=(
             jax.ShapeDtypeStruct((chan_rows, block), jnp.bfloat16),
             jax.ShapeDtypeStruct((chan_rows, block), jnp.bfloat16),
-            jax.ShapeDtypeStruct((everyone, groups, block), jnp.float32),
+            jax.ShapeDtypeStruct(filters.shape, jnp.float32),
         ),
-        in_specs=[vmem] * 4,
+        in_specs=[hbm, hbm, hbm, vmem],
         out_specs=(vmem, vmem, vmem),
         scratch_shapes=[
+            pltpu.VMEM((chan_rows, block), jnp.bfloat16),
+            pltpu.VMEM((chan_rows, block), jnp.bfloat16),
+            pltpu.VMEM((chan_count * peers, groups, block), jnp.float32),
+            pltpu.VMEM((everyone, groups, block), jnp.float32),
             pltpu.VMEM((chan_rows, block), jnp.bfloat16),
             pltpu.VMEM((groups, rows, TILE), jnp.bfloat16),
             pltpu.VMEM((groups, 2 * rows, TILE), jnp.bfloat16),
@@ -613,15 +645,12 @@
         + [pair] * 8
         + [stacked] * 2
         + [single] * 2
-        + [many] * 4,
+        + [many] * 4
+        + [pltpu.SemaphoreType.DMA((2,))],
         compiler_params=pltpu.CompilerParams(
             collective_id=0, has_side_effects=True, vmem_limit_bytes=40 * 1024 * 1024
         ),
-    )(inputs, gating, grad_out, packed)
-    grads = grads.reshape(chan_count, LAYERS, peers * groups, block).sum(axis=1)
-    grads = grads.reshape(G, block)
-    grad_filters = lax.dynamic_slice_in_dim(grads, chan * share, share, 1)
-    return (grad_inputs, grad_gating, grad_filters)
+    )(inputs, gating, grad_out, filters)
 
 
 def solution(mesh):

time: 67 us -> 61.9 us (0.924)
  Pallas kernels: 59.6 us -> 54.9 us
  other arithmetic: 0.8 us -> 0 us
    pallas_call x1, Pallas kernels: 59.6 us -> 54.9 us  [layered_shards(): pl.pallas_call(functools.partial(layered_kernel, seq_count, chan_count),...]
    unnamed x8 -> x11, local copies, waits for them, and re-layouts: 4.7 us -> 6.08 us
    mul x1 -> x0, other arithmetic: 0.76 us -> none  [layered_shards(): lanes = jnp.tile(filters * factor, (1, chan_count))]
    dynamic_slice x1 -> x0, local copies, waits for them, and re-layouts: 0.7 us -> none  [layered_shards(): grad_filters = lax.dynamic_slice_in_dim(grads, chan * share, share, 1)]
where the time goes in v3:
time: 61.9 us; the launch traced here: 61.6 us
  Pallas kernels  54.9 us (89%)
  local copies, waits for them, and re-layouts  6.08 us (10%)
  between operations  0.65 us (1%)
    pallas_call x1, Pallas kernels, layered_shards(): pl.pallas_call(functools.partial(layered_kernel, seq_count, chan_count),...  54.9 us
    unnamed x11, local copies, waits for them, and re-layouts  6.08 us

profile of v3, /device:TPU:0, one launch (start us, length us, event | category | flops | bytes accessed | tf_op | source)
XLA Modules:
  0.0 61.6 jit_solution(5145464958009732059)
XLA Ops:
  0.6 0.0 copy-start
  0.6 1.0 %copy-done = bf16[2048,128]{1,0:T(8,128)(2,1)S(1)} copy-done((bf16[2048,128]{1,0:T(8,128)(2,1)S(1)}, bf16[2048,128]{1,0:T(8,128)(2,1)}, u32[]{:S(2)}) %copy-start) | copy-done | bytes 524312
  1.7 0.0 copy-start.1
  1.7 1.0 %copy-done.1 = bf16[2048,128]{1,0:T(8,128)(2,1)S(1)} copy-done((bf16[2048,128]{1,0:T(8,128)(2,1)S(1)}, bf16[2048,128]{1,0:T(8,128)(2,1)}, u32[]{:S(2)}) %copy-start.1) | copy-done | bytes 524312
  2.7 0.0 copy-start.2
  2.7 1.0 %copy-done.2 = bf16[2048,128]{1,0:T(8,128)(2,1)S(1)} copy-done((bf16[2048,128]{1,0:T(8,128)(2,1)S(1)}, bf16[2048,128]{1,0:T(8,128)(2,1)}, u32[]{:S(2)}) %copy-start.2) | copy-done | bytes 524312
  3.8 0.0 copy-start.3
  3.8 0.8 %copy-done.3 = f32[64,64]{1,0:T(8,128)S(1)} copy-done((f32[64,64]{1,0:T(8,128)S(1)}, f32[64,64]{1,0:T(8,128)}, u32[]{:S(2)}) %copy-start.3) | copy-done | bytes 16408
  4.5 54.9 %shard_map.67 = (bf16[2048,128]{1,0:T(8,128)(2,1)S(1)}, bf16[2048,128]{1,0:T(8,128)(2,1)S(1)}, f32[64,64]{1,0:T(8,128)S(1)}) custom-call(bf16[2048,128]{1,0:T(8,128)(2,1)S(1)} %copy-done, bf16[2048,128]{1,0:T(8,128)(2,1)S(1)} %copy-done.1, bf16[2048,128]{1,0:T(8,128)(2,1)S(1)} %copy-done.2, f32[64,64]{1,0:T(8,128)S(1)} %copy-done.3), custom_call_target="tpu_custom_call" | custom-call | tf_op jit(solution)/shard_map/pallas_call | solution.py:617
  59.4 0.8 %copy.10 = bf16[2048,128]{1,0:T(8,128)(2,1)} copy(bf16[2048,128]{1,0:T(8,128)(2,1)S(1)} %get-tuple-element.6) | data formatting | bytes 1048576
  60.2 0.8 %copy.11 = bf16[2048,128]{1,0:T(8,128)(2,1)} copy(bf16[2048,128]{1,0:T(8,128)(2,1)S(1)} %get-tuple-element.7) | data formatting | bytes 1048576
  61.0 0.6 copy.12
Async XLA Ops:
  0.6 1.0 %copy-start = (bf16[2048,128]{1,0:T(8,128)(2,1)S(1)}, bf16[2048,128]{1,0:T(8,128)(2,1)}, u32[]{:S(2)}) copy-start(bf16[2048,128]{1,0:T(8,128)(2,1)} %x_ref.1) | copy-start | bytes 1572868
  1.7 1.0 %copy-start.1 = (bf16[2048,128]{1,0:T(8,128)(2,1)S(1)}, bf16[2048,128]{1,0:T(8,128)(2,1)}, u32[]{:S(2)}) copy-start(bf16[2048,128]{1,0:T(8,128)(2,1)} %gate_hbm.1) | copy-start | bytes 1572868
  2.7 1.0 %copy-start.2 = (bf16[2048,128]{1,0:T(8,128)(2,1)S(1)}, bf16[2048,128]{1,0:T(8,128)(2,1)}, u32[]{:S(2)}) copy-start(bf16[2048,128]{1,0:T(8,128)(2,1)} %up_hbm.1) | copy-start | bytes 1572868
  3.8 0.8 %copy-start.3 = (f32[64,64]{1,0:T(8,128)S(1)}, f32[64,64]{1,0:T(8,128)}, u32[]{:S(2)}) copy-start(f32[64,64]{1,0:T(8,128)} %raw_ref.1) | copy-start | bytes 49156
